TPU v7x, 512 devices: a whole 4x4x16 slice. The times are simulated.
512 devices in a mesh: dp: 64 (over z, x_hi, core), mp: 8 (over x_lo, y).
Axes of the slice: x: 4 (x_hi: 2, x_lo: 2; x = x_hi * 2 + x_lo), y: 4, z: 16, core: 2. Of those that a mesh axis runs over, the one named last changes fastest.
Arguments:
- normed_input_rows: bfloat16 [24576, 8192], P('dp', 'mp'), may hold values from -6 to 6
- frozen_queries: bfloat16 [24576, 8192], P('dp', 'mp'), may hold values from -6 to 6
- frozen_keys: bfloat16 [24576, 1024], P('dp', 'mp'), may hold values from -6 to 6
- frozen_values: bfloat16 [24576, 1024], P('dp', 'mp'), may hold values from -6 to 6
- attention_output_gradient: bfloat16 [24576, 8192], P('dp', 'mp'), may hold values from -1.1953125 to 1.1953125
- adapter_down_weight: float32 [64, 8192, 192], P(None, ('mp', 'dp')), may hold values from -0.0625 to 0.0625
- adapter_up_query: float32 [64, 64, 8192], P(None, 'dp', 'mp'), may hold values from -0.75 to 0.75
- adapter_up_key_value: float32 [64, 64, 8, 256], P(None, 'dp', 'mp'), may hold values from -0.75 to 0.75
- document_numbers: int32 [24576], P('dp'), may hold values from 0 to 1535, as said below
- block_tenant_slot: int32 [192], P('dp'), may hold values from 0 to 1, as said below
- shard_tenant_table: int32 [64, 2], replicated, may hold values from 0 to 63, as said below
Outputs:
- grad_down: float32 [64, 8192, 192], P(None, ('mp', 'dp'))
- grad_upq: float32 [64, 64, 8192], P(None, 'dp', 'mp')
- grad_upkv: float32 [64, 64, 8, 256], P(None, 'dp', 'mp')
Inputs may be any that keep to these rules, and one draw needn't show every extreme that they name: `document_numbers`: document numbers never fall along the rows; a document starts only at a multiple of 16 rows, always at the first row of each index of dp, at the last 16 rows of all, and wherever the slot of a block changes; a document's number is its first row divided by 16. `block_tenant_slot`: the 3 blocks of each index of dp name slots in an order that never falls, and every one of the 2 slots is named. `shard_tenant_table`: each row holds 2 distinct tenants.
All inputs are finite; a program needn't handle non-finite values.
Results may differ from a plain program's by a relative error of at most 0.012.
The roundings to bfloat16 on the way count: a program that leaves them out, or rounds other values in their place, can miss the bound.
Values sent between devices are 32-bit elements; how exact they have to be, the bound alone decides.
A program may use at most 64 MiB of HBM per device.

v0:
```python
import jax
import jax.numpy as jnp
from jax import lax
from jax.sharding import PartitionSpec as P

ADAPTER_SCALE = 0.5
MASKED = -1e30
PRECISION_HIGH = lax.Precision.HIGHEST


def attention_grads(query_row_block, key_row_block, value_row_block, upstream, doc_row):
    row_total = query_row_block.shape[0]
    kv_heads = key_row_block.shape[1]
    groups = query_row_block.shape[1] // kv_heads
    head_size = query_row_block.shape[2]
    query_g = query_row_block.reshape(row_total, kv_heads, groups, head_size)
    upstream_g = upstream.reshape(row_total, kv_heads, groups, head_size)
    inverse = 1.0 / head_size**0.5
    scores = (
        jnp.einsum("qkgd,jkd->kgqj", query_g, key_row_block, preferred_element_type=jnp.float32)
        * inverse
    )
    position = jnp.arange(row_total, dtype=jnp.int32)
    allowed = (doc_row[:, None] == doc_row[None, :]) & (position[:, None] >= position[None, :])
    scores = jnp.where(allowed, scores, MASKED)
    row_top = jnp.max(scores, axis=-1, keepdims=True)
    weights = jnp.exp(scores - row_top)
    attn_probs = weights / jnp.sum(weights, axis=-1, keepdims=True)
    probs_low = attn_probs.astype(jnp.bfloat16)
    grad_probs = jnp.einsum(
        "qkgd,jkd->kgqj", upstream_g, value_row_block, preferred_element_type=jnp.float32
    )
    row_inner = jnp.sum(attn_probs * grad_probs, axis=-1, keepdims=True)
    grad_scores = (attn_probs * (grad_probs - row_inner) * inverse).astype(jnp.bfloat16)
    grad_query = jnp.einsum(
        "kgqj,jkd->qkgd", grad_scores, key_row_block, preferred_element_type=jnp.float32
    ).reshape(row_total, -1)
    key_gradient = jnp.einsum(
        "kgqj,qkgd->jkd", grad_scores, query_g, preferred_element_type=jnp.float32
    ).reshape(row_total, -1)
    value_gradient = jnp.einsum(
        "kgqj,qkgd->jkd", probs_low, upstream_g, preferred_element_type=jnp.float32
    ).reshape(row_total, -1)
    return (grad_query, key_gradient, value_gradient)


def adapted(frozen_rows, low_part, panel_cols):
    extra_term = jnp.einsum("brk,bkc->brc", low_part, panel_cols, precision=PRECISION_HIGH)
    extra_term = extra_term.reshape(frozen_rows.shape[0], -1)
    return (frozen_rows.astype(jnp.float32) + ADAPTER_SCALE * extra_term).astype(jnp.bfloat16)


def on_device(
    normed_input_rows,
    frozen_queries,
    frozen_keys,
    frozen_values,
    attention_output_gradient,
    adapter_down_weight,
    adapter_up_query,
    adapter_up_key_value,
    document_numbers,
    block_tenant_slot,
    shard_tenant_table,
):
    row_count = normed_input_rows.shape[0]
    block_count = block_tenant_slot.shape[0]
    block_rows = row_count // block_count
    dp_count = lax.axis_size("dp")
    count_of_tenants = adapter_down_weight.shape[0]
    desired_result = shard_tenant_table.reshape(-1)
    down_panels, upq_panels, upkv_panels = (
        lax.all_to_all(
            adapter_down_weight[desired_result], "dp", split_axis=0, concat_axis=1, tiled=True
        ),
        lax.all_to_all(
            adapter_up_query[desired_result], "dp", split_axis=0, concat_axis=1, tiled=True
        ),
        lax.all_to_all(
            adapter_up_key_value[desired_result], "dp", split_axis=0, concat_axis=1, tiled=True
        ),
    )
    adapter_rank = down_panels.shape[2] // 3
    row_blocks = normed_input_rows.reshape(block_count, block_rows, -1).astype(jnp.float32)
    partial_down = jnp.einsum(
        "bri,bij->brj", row_blocks, down_panels[block_tenant_slot], precision=PRECISION_HIGH
    )
    lowrank = lax.psum(partial_down.reshape(row_count, 3 * adapter_rank), "mp")
    head_size = upkv_panels.shape[3] // 2
    kv_heads = upkv_panels.shape[2]
    query_heads = frozen_queries.shape[1] // head_size
    low_blocks = lowrank.reshape(block_count, block_rows, 3, adapter_rank)
    upq_blocks = upq_panels[block_tenant_slot]
    upkv_blocks = upkv_panels[block_tenant_slot]
    upk_blocks = upkv_blocks[..., :head_size].reshape(
        block_count, adapter_rank, kv_heads * head_size
    )
    upv_blocks = upkv_blocks[..., head_size:].reshape(
        block_count, adapter_rank, kv_heads * head_size
    )
    query_row_block = adapted(frozen_queries, low_blocks[:, :, 0], upq_blocks)
    key_row_block = adapted(frozen_keys, low_blocks[:, :, 1], upk_blocks)
    value_row_block = adapted(frozen_values, low_blocks[:, :, 2], upv_blocks)
    grad_query, key_gradient, value_gradient = attention_grads(
        query_row_block.reshape(row_count, query_heads, head_size),
        key_row_block.reshape(row_count, kv_heads, head_size),
        value_row_block.reshape(row_count, kv_heads, head_size),
        attention_output_gradient.reshape(row_count, query_heads, head_size),
        document_numbers,
    )
    gq_blocks = grad_query.reshape(block_count, block_rows, -1)
    gk_blocks = key_gradient.reshape(block_count, block_rows, -1)
    gv_blocks = value_gradient.reshape(block_count, block_rows, -1)
    gradient_portion = ADAPTER_SCALE * jnp.concatenate(
        [
            jnp.einsum("brc,bkc->brk", gq_blocks, upq_blocks, precision=PRECISION_HIGH),
            jnp.einsum("brc,bkc->brk", gk_blocks, upk_blocks, precision=PRECISION_HIGH),
            jnp.einsum("brc,bkc->brk", gv_blocks, upv_blocks, precision=PRECISION_HIGH),
        ],
        axis=-1,
    )
    lowrank_grad = lax.psum(gradient_portion.reshape(row_count, 3 * adapter_rank), "mp")
    lowrank_gradient = lowrank_grad.reshape(block_count, block_rows, 3 * adapter_rank)
    down_terms = jnp.einsum("bri,brj->bij", row_blocks, lowrank_gradient, precision=PRECISION_HIGH)
    query_up_terms = ADAPTER_SCALE * jnp.einsum(
        "brk,brc->bkc", low_blocks[:, :, 0], gq_blocks, precision=PRECISION_HIGH
    )
    key_up_terms = ADAPTER_SCALE * jnp.einsum(
        "brk,brc->bkc", low_blocks[:, :, 1], gk_blocks, precision=PRECISION_HIGH
    )
    value_up_terms = ADAPTER_SCALE * jnp.einsum(
        "brk,brc->bkc", low_blocks[:, :, 2], gv_blocks, precision=PRECISION_HIGH
    )
    upkv_terms = jnp.concatenate(
        [
            key_up_terms.reshape(block_count, adapter_rank, kv_heads, head_size),
            value_up_terms.reshape(block_count, adapter_rank, kv_heads, head_size),
        ],
        axis=-1,
    )
    all_slots = lax.all_gather(block_tenant_slot, "dp", axis=0, tiled=True)
    senders = jnp.arange(dp_count * block_count, dtype=jnp.int32) // block_count
    owners = shard_tenant_table[senders, all_slots]
    down_in, upq_in, upkv_in = (
        lax.all_to_all(down_terms, "dp", split_axis=1, concat_axis=0, tiled=True),
        lax.all_to_all(query_up_terms, "dp", split_axis=1, concat_axis=0, tiled=True),
        lax.all_to_all(upkv_terms, "dp", split_axis=1, concat_axis=0, tiled=True),
    )
    owner_hot = (jnp.arange(count_of_tenants, dtype=jnp.int32)[:, None] == owners[None, :]).astype(
        jnp.float32
    )
    grad_down = jnp.einsum("tj,jrc->trc", owner_hot, down_in, precision=PRECISION_HIGH)
    grad_upq = jnp.einsum("tj,jrc->trc", owner_hot, upq_in, precision=PRECISION_HIGH)
    grad_upkv = jnp.einsum("tj,jrkc->trkc", owner_hot, upkv_in, precision=PRECISION_HIGH)
    return (grad_down, grad_upq, grad_upkv)


def solution(mesh):
    placed = (
        P("dp", "mp"),
        P("dp", "mp"),
        P("dp", "mp"),
        P("dp", "mp"),
        P("dp", "mp"),
        P(None, ("mp", "dp"), None),
        P(None, "dp", "mp"),
        P(None, "dp", "mp", None),
        P("dp"),
        P("dp"),
        P(),
    )
    return jax.shard_map(
        on_device,
        mesh=mesh,
        in_specs=placed,
        out_specs=(P(None, ("mp", "dp"), None), P(None, "dp", "mp"), P(None, "dp", "mp", None)),
        check_vma=False,
    )
```

profile of v0, /device:TPU:1, one launch (start us, length us, event | category | flops | bytes accessed | tf_op | source)
XLA Modules:
  0.0 653.4 jit_solution(5255772222505822899)
XLA Ops:
  10.6 19.6 %all-to-all-start.1 = ((f32[128,1,1,256]{3,2,1,0:T(1,128)}), f32[128,1,1,256]{3,2,1,0:T(1,128)S(1)}, u32[]{:S(2)}, u32[]{:S(2)}) async-start(f32[128,1,1,256]{3,2,1,0:T(1,128)} %copy.147), calls=%async_computation.1 | async-start | bytes 262144 | tf_op jit(solution)/shard_map/all_to_all | solution.py:79
  30.2 2.1 gather_fusion.1
  32.4 16.5 %all-to-all-done.1 = f32[128,1,1,256]{3,2,1,0:T(1,128)S(1)} async-done(((f32[128,1,1,256]{3,2,1,0:T(1,128)}), f32[128,1,1,256]{3,2,1,0:T(1,128)S(1)}, u32[]{:S(2)}, u32[]{:S(2)}) %all-to-all-start.1) | async-done | bytes 131104 | tf_op jit(solution)/shard_map/all_to_all | solution.py:79
  48.8 4.5 all-to-all-start
  55.6 96.2 %all-to-all-done = f32[128,16,192]{2,1,0:T(8,128)S(1)} async-done(((f32[128,16,192]{2,1,0:T(8,128)}), f32[128,16,192]{2,1,0:T(8,128)S(1)}, u32[]{:S(2)}, u32[]{:S(2)}) %all-to-all-start) | async-done | bytes 1572896 | tf_op jit(solution)/shard_map/all_to_all | solution.py:73
  151.8 8.2 %all-to-all-start.2 = ((f32[128,1,1024]{2,1,0:T(1,128)}), f32[128,1,1024]{2,1,0:T(1,128)}, u32[]{:S(2)}, u32[]{:S(2)}) async-start(f32[128,1,1024]{2,1,0:T(1,128)} %copy.149), calls=%async_computation.2 | async-start | bytes 1048576 | tf_op jit(solution)/shard_map/all_to_all | solution.py:76
  166.0 2.9 fusion.45
  170.4 23.6 %all-to-all-done.2 = f32[128,1,1024]{2,1,0:T(1,128)} async-done(((f32[128,1,1024]{2,1,0:T(1,128)}), f32[128,1,1024]{2,1,0:T(1,128)}, u32[]{:S(2)}, u32[]{:S(2)}) %all-to-all-start.2) | async-done | bytes 524320 | tf_op jit(solution)/shard_map/all_to_all | solution.py:76
  195.8 59.5 %all-reduce.4.cloned.1.call-done = f32[3,128,3,64]{1,3,0,2:T(8,128)} async-done(((f32[3,128,3,64]{1,3,0,2:T(8,128)}), f32[3,128,3,64]{1,3,0,2:T(8,128)}) %all-reduce.4.cloned.1.call-update) | async-done | bytes 294928 | tf_op jit(solution)/shard_map/psum | solution.py:88
  256.7 2.3 convolution_multiply_fusion
  267.9 2.9 copy.157
  271.0 2.3 convolution_bitcast_fusion.3
  276.8 20.7 %all-to-all-start.5 = ((f32[3,64,1,256]{3,2,0,1:T(1,128)}), f32[3,64,1,256]{3,2,0,1:T(1,128)}, u32[]{:S(2)}, u32[]{:S(2)}) async-start(f32[3,64,1,256]{3,2,0,1:T(1,128)} %copy.168), calls=%async_computation.5 | async-start | bytes 393216 | tf_op jit(solution)/shard_map/all_to_all | solution.py:147
  299.3 3.0 copy.155
  307.3 11.2 %all-to-all-done.5 = f32[3,64,1,256]{3,2,0,1:T(1,128)} async-done(((f32[3,64,1,256]{3,2,0,1:T(1,128)}), f32[3,64,1,256]{3,2,0,1:T(1,128)}, u32[]{:S(2)}, u32[]{:S(2)}) %all-to-all-start.5) | async-done | bytes 196640 | tf_op jit(solution)/shard_map/all_to_all | solution.py:147
  318.5 5.1 all-to-all-start.4
  327.3 83.9 %all-reduce.6.cloned.1.call-done = f32[3,128,192]{1,2,0:T(8,128)} async-done(((f32[3,128,192]{1,2,0:T(8,128)}), f32[3,128,192]{1,2,0:T(8,128)}) %all-reduce.6.cloned.1.call-update) | async-done | bytes 294928 | tf_op jit(solution)/shard_map/psum | solution.py:122
  411.2 2.3 convolution_bitcast_fusion
  413.5 3.2 copy.163
  416.7 20.8 %all-to-all-start.3 = ((f32[3,1024,192]{2,0,1:T(4,128)}), f32[3,1024,192]{2,0,1:T(4,128)}, u32[]{:S(2)}, u32[]{:S(2)}) async-start(f32[3,1024,192]{2,0,1:T(4,128)} %copy.163), calls=%async_computation.3 | async-start | bytes 8388608 | tf_op jit(solution)/shard_map/all_to_all | solution.py:145
  439.7 191.5 %all-reduce = s32[192]{0:T(256)S(1)} all-reduce(s32[192]{0:T(256)S(1)} %dynamic-update-slice), channel_id=1, replica_groups=mesh['dp'=64,'mp'=8] {'dp'}, use_global_device_ids=true, to_apply=%add | all-reduce | flops 192 | bytes 1536
  631.3 2.2 gather_fusion
  638.6 2.8 copy.164
  641.8 3.2 fusion.7
  (100 shorter events, 47.5 us)
Async XLA Ops:
  7.2 23.1 %copy-start = (f32[64,16,192]{2,1,0:T(8,128)S(1)}, f32[64,16,192]{2,1,0:T(8,128)}, u32[]{:S(2)}) copy-start(f32[64,16,192]{2,1,0:T(8,128)} %param.16) | copy-start | bytes 2359300
  10.6 38.2 %all-to-all-start.1 = ((f32[128,1,1,256]{3,2,1,0:T(1,128)}), f32[128,1,1,256]{3,2,1,0:T(1,128)S(1)}, u32[]{:S(2)}, u32[]{:S(2)}) async-start(f32[128,1,1,256]{3,2,1,0:T(1,128)} %copy.147), calls=%async_computation.1 | async-start | bytes 262144 | tf_op jit(solution)/shard_map/all_to_all | solution.py:79
  30.2 23.1 %copy-start.10 = (f32[64,1,1024]{2,1,0:T(1,128)S(1)}, f32[64,1,1024]{2,1,0:T(1,128)}, u32[]{:S(2)}) copy-start(f32[64,1,1024]{2,1,0:T(1,128)} %param.17) | copy-start | bytes 786436
  48.8 103.0 %all-to-all-start = ((f32[128,16,192]{2,1,0:T(8,128)}), f32[128,16,192]{2,1,0:T(8,128)S(1)}, u32[]{:S(2)}, u32[]{:S(2)}) async-start(f32[128,16,192]{2,1,0:T(8,128)} %gather_fusion.1), calls=%async_computation | async-start | bytes 4194304 | tf_op jit(solution)/shard_map/all_to_all | solution.py:73
  53.4 106.9 %copy-start.15 = (s32[3]{0:T(128)S(1)}, s32[3]{0:T(128)}, u32[]{:S(2)}) copy-start(s32[3]{0:T(128)} %param.20) | copy-start | bytes 40
  151.8 42.1 %all-to-all-start.2 = ((f32[128,1,1024]{2,1,0:T(1,128)}), f32[128,1,1024]{2,1,0:T(1,128)}, u32[]{:S(2)}, u32[]{:S(2)}) async-start(f32[128,1,1024]{2,1,0:T(1,128)} %copy.149), calls=%async_computation.2 | async-start | bytes 1048576 | tf_op jit(solution)/shard_map/all_to_all | solution.py:76
  160.0 95.2 %all-reduce.4.cloned.1.call-start = ((), (), s32[]{:S(2)}) async-start(), calls=%async_computation.6 | async-start | bytes 589824 | tf_op jit(solution)/shard_map/psum | solution.py:88
  161.8 4.1 copy-start.5
  163.8 5.8 copy-start.13
  166.0 90.7 %copy-start.11 = (bf16[384,128]{1,0:T(8,128)(2,1)S(1)}, bf16[384,128]{1,0:T(8,128)(2,1)}, u32[]{:S(2)}) copy-start(bf16[384,128]{1,0:T(8,128)(2,1)} %param.13) | copy-start | bytes 294916
  168.9 90.1 %copy-start.9 = (bf16[384,1024]{1,0:T(8,128)(2,1)S(1)}, bf16[384,1024]{1,0:T(8,128)(2,1)}, u32[]{:S(2)}) copy-start(bf16[384,1024]{1,0:T(8,128)(2,1)} %param.12) | copy-start | bytes 2359300
  170.4 90.9 %copy-start.6 = (f32[3,64,256]{2,1,0:T(8,128)}, f32[3,64,256]{2,1,0:T(8,128)S(1)}, u32[]{:S(2)}) copy-start(f32[3,64,256]{2,1,0:T(8,128)S(1)} %gather_fusion.4) | copy-start | bytes 589828
  195.8 60.9 %copy-start.3 = (f32[3,64,1024]{2,1,0:T(8,128)}, f32[3,64,1024]{2,1,0:T(8,128)S(1)}, u32[]{:S(2)}) copy-start(f32[3,64,1024]{2,1,0:T(8,128)S(1)} %gather_fusion.6) | copy-start | bytes 2359300
  259.3 3.3 copy-start.12
  260.2 2.4 copy-start.14
  276.8 41.7 %all-to-all-start.5 = ((f32[3,64,1,256]{3,2,0,1:T(1,128)}), f32[3,64,1,256]{3,2,0,1:T(1,128)}, u32[]{:S(2)}, u32[]{:S(2)}) async-start(f32[3,64,1,256]{3,2,0,1:T(1,128)} %copy.168), calls=%async_computation.5 | async-start | bytes 393216 | tf_op jit(solution)/shard_map/all_to_all | solution.py:147
  302.3 21.4 %copy-start.4 = (f32[3,64,1024]{2,1,0:T(8,128)S(1)}, f32[3,64,1024]{2,1,0:T(8,128)}, u32[]{:S(2)}) copy-start(f32[3,64,1024]{2,1,0:T(8,128)} %copy-done.3) | copy-start | bytes 2359300
  303.9 21.6 %copy-start.7 = (f32[3,64,256]{2,1,0:T(8,128)S(1)}, f32[3,64,256]{2,1,0:T(8,128)}, u32[]{:S(2)}) copy-start(f32[3,64,256]{2,1,0:T(8,128)} %copy-done.6) | copy-start | bytes 589828
  303.9 22.1 %copy-start.8 = (f32[384,128,1]{1,0,2:T(8,128)S(1)}, f32[384,128,1]{1,0,2:T(8,128)}, u32[]{:S(2)}) copy-start(f32[384,128,1]{1,0,2:T(8,128)} %fusion.10) | copy-start | bytes 589828
  318.5 98.2 %all-to-all-start.4 = ((f32[3,64,1024]{2,0,1:T(4,128)}), f32[3,64,1024]{2,0,1:T(4,128)}, u32[]{:S(2)}, u32[]{:S(2)}) async-start(f32[3,64,1024]{2,0,1:T(4,128)} %copy.167), calls=%async_computation.4 | async-start | bytes 2097152 | tf_op jit(solution)/shard_map/all_to_all | solution.py:146
  323.6 87.6 %all-reduce.6.cloned.1.call-start = ((), (), s32[]{:S(2)}) async-start(), calls=%async_computation.7 | async-start | bytes 589824 | tf_op jit(solution)/shard_map/psum | solution.py:122
  416.7 214.6 %copy-start.2 = (s32[64,2]{0,1:T(2,128)S(1)}, s32[64,2]{0,1:T(2,128)}, u32[]{:S(2)}) copy-start(s32[64,2]{0,1:T(2,128)} %param.21) | copy-start | bytes 1540
  416.7 221.9 %all-to-all-start.3 = ((f32[3,1024,192]{2,0,1:T(4,128)}), f32[3,1024,192]{2,0,1:T(4,128)}, u32[]{:S(2)}, u32[]{:S(2)}) async-start(f32[3,1024,192]{2,0,1:T(4,128)} %copy.163), calls=%async_computation.3 | async-start | bytes 8388608 | tf_op jit(solution)/shard_map/all_to_all | solution.py:145
  641.4 5.1 copy-start.1
Sparse Core Ops, SparseCore 0:
  169.8 85.4 all-reduce.3
  327.6 83.5 all-reduce.5
where the time goes:
time: 656 us; the launch traced here: 653 us
  waiting for transfers between devices  291 us (44%)
  blocking collectives  192 us (29%)
  starting transfers between devices  79.2 us (12%)
  local copies, waits for them, and re-layouts  42.8 us (7%)
  matrix products  29.8 us (5%)
  between operations  15.3 us (2%)
    unnamed x1, blocking collectives  192 us
    all_to_all x1, waiting for transfers between devices, on_device(): lax.all_to_all(adapter_down_weight[desired_result], 'dp', split_axis=0, c...  96.2 us
    psum x1, waiting for transfers between devices, on_device(): lax.psum(gradient_portion.reshape(row_count, 3 * adapter_rank), 'mp')  83.9 us
    psum x1, waiting for transfers between devices, on_device(): lowrank = lax.psum(partial_down.reshape(row_count, 3 * adapter_rank), 'mp')  59.5 us
    all_to_all x1, waiting for transfers between devices, on_device(): lax.all_to_all(adapter_up_query[desired_result], 'dp', split_axis=0, conc...  23.6 us
    all_to_all x1, starting transfers between devices, on_device(): lax.all_to_all(down_terms, 'dp', split_axis=1, concat_axis=0, tiled=True)  20.8 us
    all_to_all x1, starting transfers between devices, on_device(): lax.all_to_all(upkv_terms, 'dp', split_axis=1, concat_axis=0, tiled=True)  20.7 us
    all_to_all x1, starting transfers between devices, on_device(): lax.all_to_all(adapter_up_key_value[desired_result], 'dp', split_axis=0,...  19.6 us
  transfers between devices with their start and end apart: 8, of which 6 were waited for; matrix products, arithmetic and copies ran while one was open for 7% of the time, Pallas kernels for 0%

commit v1 on v0

v1 whole, which is shorter than its diff:
```python
import functools

import jax
import jax.numpy as jnp
from jax import lax
from jax.experimental import pallas as pl
from jax.experimental.pallas import tpu as pltpu
from jax.sharding import PartitionSpec as P

ADAPTER_SCALE = 0.5
MASKED = -1e30
MESH = pl.DeviceIdType.MESH
LANES = 128
F32 = jnp.float32
BF16 = jnp.bfloat16


def dot(a, b, ca, cb):
    return lax.dot_general(a, b, (((ca,), (cb,)), ((), ())), preferred_element_type=F32)


def parts(a):
    high = a.astype(BF16)
    return high, (a - high.astype(F32)).astype(BF16)


def dot_exact_left(a, b, ca, cb):
    high, low = parts(b)
    return dot(a, high, ca, cb) + dot(a, low, ca, cb)


def dot_both(a, b, ca, cb):
    a_high, a_low = parts(a)
    b_high, b_low = parts(b)
    return dot(a_high, b_high, ca, cb) + (dot(a_high, b_low, ca, cb) + dot(a_low, b_high, ca, cb))


def barrier(dp, mp, n_dp, n_mp):
    sem = pltpu.get_barrier_semaphore()

    @pl.loop(1, n_dp)
    def _(k):
        pl.semaphore_signal(
            sem, inc=1, device_id={"dp": lax.rem(dp + k, n_dp)}, device_id_type=MESH
        )

    for k in range(1, n_mp):
        pl.semaphore_signal(
            sem, inc=1, device_id={"mp": lax.rem(mp + k, n_mp)}, device_id_type=MESH
        )
    return lambda: pl.semaphore_wait(sem, n_dp - 1 + n_mp - 1)


class Exchange:
    def __init__(self, source, target, send, recv, dp, n_dp):
        self.source, self.target, self.send, self.recv = source, target, send, recv
        self.dp, self.n_dp = dp, n_dp

    def piece(self, k, peer, slot):
        return pltpu.make_async_remote_copy(
            src_ref=self.source.at[peer],
            dst_ref=self.target.at[slot],
            send_sem=self.send.at[k],
            recv_sem=self.recv.at[k],
            device_id={"dp": peer},
            device_id_type=MESH,
        )

    def start(self, k):
        self.piece(k, lax.rem(self.dp + k, self.n_dp), self.dp).start()

    def keep(self):
        self.target[pl.ds(self.dp, 1)] = self.source[pl.ds(self.dp, 1)]

    def wait_recv(self):
        @pl.loop(1, self.n_dp)
        def _(k):
            origin = lax.rem(self.dp + self.n_dp - k, self.n_dp)
            self.piece(k, origin, origin).wait_recv()

    def wait_send(self):
        @pl.loop(1, self.n_dp)
        def _(k):
            self.piece(k, lax.rem(self.dp + k, self.n_dp), self.dp).wait_send()


def start_all(exchanges, n_dp):
    for group in exchanges:

        @pl.loop(0, n_dp - 1)
        def _(i):
            half = lax.div(i + 2, 2)
            k = jnp.where(lax.rem(i, 2) == 0, half, n_dp - half)
            for exchange in group:
                exchange.start(k)


class SumOverMp:
    def __init__(self, partial, landed, total, sems, mp, n_mp):
        self.partial, self.landed, self.total = partial, landed, total
        self.mp, self.n_mp = mp, n_mp
        self.rows = partial.shape[0] // n_mp
        self.sems = sems

    def rows_of(self, p):
        return pl.ds(pl.multiple_of(p * self.rows, 8), self.rows)

    def copy(self, k, second):
        peer = lax.rem(self.mp + k, self.n_mp)
        if second:
            source = target = self.total.at[self.rows_of(self.mp)]
        else:
            source, target = self.partial.at[self.rows_of(peer)], self.landed.at[k]
        return pltpu.make_async_remote_copy(
            src_ref=source,
            dst_ref=target,
            send_sem=self.sems.at[2 * second, k],
            recv_sem=self.sems.at[2 * second + 1, k],
            device_id={"mp": peer},
            device_id_type=MESH,
        )

    def landed_total(self, k):
        origin = lax.rem(self.mp + self.n_mp - k, self.n_mp)
        return pltpu.make_async_remote_copy(
            src_ref=self.total.at[self.rows_of(origin)],
            dst_ref=self.total.at[self.rows_of(origin)],
            send_sem=self.sems.at[2, k],
            recv_sem=self.sems.at[3, k],
            device_id={"mp": origin},
            device_id_type=MESH,
        )

    def run(self):
        for k in range(1, self.n_mp):
            self.copy(k, 0).start()
        mine = self.partial[self.rows_of(self.mp)]
        for k in range(1, self.n_mp):
            self.copy(k, 0).wait_recv()
            mine = mine + self.landed[k]
        self.total[self.rows_of(self.mp)] = mine
        for k in range(1, self.n_mp):
            self.copy(k, 1).start()
        for k in range(1, self.n_mp):
            self.landed_total(k).wait_recv()

    def finish(self):
        for k in range(1, self.n_mp):
            self.copy(k, 0).wait_send()
            self.copy(k, 1).wait_send()


def store_packed(ref, wide, narrow):
    rows = wide.shape[0]
    half = rows // 2
    ref[0:rows] = wide
    ref[rows : rows + half] = jnp.concatenate([narrow[0:half], narrow[half:rows]], axis=1)


def load_packed(ref, rows):
    half = rows // 2
    tail = ref[rows : rows + half]
    width = tail.shape[1] // 2
    return ref[0:rows], jnp.concatenate([tail[:, :width], tail[:, width:]], axis=0)


def whole_kernel(
    n_dp,
    n_mp,
    rows_ref,
    queries_ref,
    keys_ref,
    values_ref,
    upstream_ref,
    down_ref,
    upq_ref,
    upkv_ref,
    slot_ref,
    doc_col_ref,
    doc_row_ref,
    table_ref,
    got_down_ref,
    got_upq_ref,
    got_upkv_ref,
    send_down,
    send_upq,
    send_upkv,
    recv_down,
    recv_upq,
    recv_upkv,
    partial,
    landed,
    total,
    partial_back,
    landed_back,
    total_back,
    bias,
    send_upq_back,
    send_upkv_back,
    send_down_back,
    exchange_sems,
    sum_sems,
):
    dp, mp = lax.axis_index("dp"), lax.axis_index("mp")
    row_total = rows_ref.shape[0]
    rank = down_ref.shape[2] // 3
    wide = 2 * rank
    columns = down_ref.shape[1]
    heads = queries_ref.shape[1] // LANES
    inverse = 1.0 / float(LANES) ** 0.5

    arrived = barrier(dp, mp, n_dp, n_mp)

    @pl.loop(0, n_dp)
    def _(d):
        first, second = table_ref[d, 0], table_ref[d, 1]
        a, b = down_ref[first], down_ref[second]
        send_down[d] = jnp.concatenate(
            [a[:, :wide], b[:, :wide], jnp.concatenate([a[:, wide:], b[:, wide:]], axis=1)],
            axis=0,
        )
        send_upq[d] = jnp.concatenate([upq_ref[first], upq_ref[second]], axis=0)
        send_upkv[d, 0:2] = upkv_ref[first]
        send_upkv[d, 2:4] = upkv_ref[second]

    arrived()

    def exchange(index, source, target):
        return Exchange(
            source, target, exchange_sems.at[2 * index], exchange_sems.at[2 * index + 1], dp, n_dp
        )

    down_in = exchange(0, send_down, recv_down)
    upkv_in = exchange(1, send_upkv, recv_upkv)
    upq_in = exchange(2, send_upq, recv_upq)
    start_all([[down_in], [upkv_in, upq_in]], n_dp)
    down_in.keep()
    upkv_in.keep()
    upq_in.keep()

    position_key = lax.broadcasted_iota(jnp.int32, (row_total, row_total), 0)
    position_query = lax.broadcasted_iota(jnp.int32, (row_total, row_total), 1)
    joined = (doc_col_ref[...] == doc_row_ref[...]) & (position_key <= position_query)
    bias[...] = jnp.where(joined, 0.0, MASKED).astype(F32)

    in_second = slot_ref[...]
    in_first = 1.0 - in_second

    down_in.wait_recv()
    rows = rows_ref[...]

    def panel(i):
        return recv_down[:, i * columns : (i + 1) * columns, :].reshape(n_dp * columns, LANES)

    low_wide = (
        dot_exact_left(rows, panel(0), 1, 0) * in_first
        + dot_exact_left(rows, panel(1), 1, 0) * in_second
    )
    both = dot_exact_left(rows, panel(2), 1, 0)
    low_narrow = both[:, :rank] * in_first[:, :rank] + both[:, rank:] * in_second[:, :rank]
    store_packed(partial, low_wide, low_narrow)
    low_sum = SumOverMp(partial, landed, total, sum_sems.at[0], mp, n_mp)
    low_sum.run()
    low_wide, low_v = load_packed(total, row_total)

    def by_slot(low):
        return jnp.concatenate(
            [low * in_first[:, :rank], low * in_second[:, :rank]], axis=1
        )

    low_q = by_slot(low_wide[:, :rank])
    low_k = by_slot(low_wide[:, rank:])
    low_v = by_slot(low_v)

    upkv_in.wait_recv()
    upq_in.wait_recv()

    up_k = jnp.concatenate([recv_upkv[:, 0, :], recv_upkv[:, 2, :]], axis=0)
    up_v = jnp.concatenate([recv_upkv[:, 1, :], recv_upkv[:, 3, :]], axis=0)

    def adapted(frozen, low, panel):
        return (frozen.astype(F32) + ADAPTER_SCALE * dot_both(low, panel, 1, 0)).astype(BF16)

    key = adapted(keys_ref[...], low_k, up_k)
    value = adapted(values_ref[...], low_v, up_v)
    low_q_parts = parts(low_q)

    def dot_low_q(grad):
        high, low = parts(grad)
        a_high, a_low = low_q_parts
        return dot(a_high, high, 0, 0) + (dot(a_high, low, 0, 0) + dot(a_low, high, 0, 0))

    grad_key = jnp.zeros((row_total, LANES), F32)
    grad_value = jnp.zeros((row_total, LANES), F32)
    grad_low_q = jnp.zeros((row_total, wide), F32)
    for head in range(heads):
        lanes = slice(head * LANES, (head + 1) * LANES)
        panel_q = jnp.concatenate(
            [recv_upq[:, head, :], recv_upq[:, heads + head, :]], axis=0
        )
        query = adapted(queries_ref[:, lanes], low_q, panel_q)
        upstream = upstream_ref[:, lanes]
        scores = dot(key, query, 1, 1) * inverse + bias[...]
        weights = jnp.exp(scores - jnp.max(scores, axis=0, keepdims=True))
        probs = weights / jnp.sum(weights, axis=0, keepdims=True)
        grad_probs = dot(value, upstream, 1, 1)
        inner = jnp.sum(probs * grad_probs, axis=0, keepdims=True)
        grad_scores = (probs * (grad_probs - inner) * inverse).astype(BF16)
        grad_key = grad_key + dot(grad_scores, query, 1, 0)
        grad_value = grad_value + dot(probs.astype(BF16), upstream, 1, 0)
        grad_head = dot(grad_scores, key, 0, 0)
        grad_low_q = grad_low_q + dot_both(grad_head, panel_q, 1, 1)
        term = ADAPTER_SCALE * dot_low_q(grad_head)
        send_upq_back[:, head, :] = term[:rank]
        send_upq_back[:, heads + head, :] = term[rank:]
    term = ADAPTER_SCALE * dot_both(low_k, grad_key, 0, 0)
    send_upkv_back[:, 0, :] = term[:rank]
    send_upkv_back[:, 2, :] = term[rank:]
    term = ADAPTER_SCALE * dot_both(low_v, grad_value, 0, 0)
    send_upkv_back[:, 1, :] = term[:rank]
    send_upkv_back[:, 3, :] = term[rank:]

    upkv_back = exchange(3, send_upkv_back, got_upkv_ref)
    upq_back = exchange(4, send_upq_back, got_upq_ref)
    down_back = exchange(5, send_down_back, got_down_ref)

    def of_slot(grad):
        return ADAPTER_SCALE * (
            grad[:, :rank] * in_first[:, :rank] + grad[:, rank:] * in_second[:, :rank]
        )

    grad_low_k = dot_both(grad_key, up_k, 1, 1)
    grad_low_v = dot_both(grad_value, up_v, 1, 1)
    store_packed(
        partial_back,
        jnp.concatenate([of_slot(grad_low_q), of_slot(grad_low_k)], axis=1),
        of_slot(grad_low_v),
    )
    start_all([[upkv_back, upq_back]], n_dp)
    upkv_back.keep()
    upq_back.keep()
    grad_sum = SumOverMp(partial_back, landed_back, total_back, sum_sems.at[1], mp, n_mp)
    grad_sum.run()
    grad_wide, grad_narrow = load_packed(total_back, row_total)

    def down_term(i, grad):
        send_down_back[:, i * columns : (i + 1) * columns, :] = dot_exact_left(
            rows, grad, 0, 0
        ).reshape(n_dp, columns, LANES)

    down_term(0, grad_wide * in_first)
    down_term(1, grad_wide * in_second)
    down_term(
        2,
        jnp.concatenate(
            [grad_narrow * in_first[:, :rank], grad_narrow * in_second[:, :rank]], axis=1
        ),
    )
    start_all([[down_back]], n_dp)
    down_back.keep()

    down_in.wait_send()
    upkv_in.wait_send()
    upq_in.wait_send()
    low_sum.finish()
    grad_sum.finish()
    for one in (upkv_back, upq_back, down_back):
        one.wait_recv()
        one.wait_send()


def owner_kernel(down_ref, upq_ref, upkv_ref, table_ref, out_down, out_upq, out_upkv):
    rank = out_down.shape[2] // 3
    wide = 2 * rank
    columns = out_down.shape[1]
    heads = out_upq.shape[1]
    out_down[...] = jnp.zeros_like(out_down)
    out_upq[...] = jnp.zeros_like(out_upq)
    out_upkv[...] = jnp.zeros_like(out_upkv)

    @pl.loop(0, down_ref.shape[0])
    def _(j):
        both = down_ref[j, 2 * columns : 3 * columns]
        for slot in range(2):
            tenant = table_ref[j, slot]
            out_down[tenant] += jnp.concatenate(
                [
                    down_ref[j, slot * columns : (slot + 1) * columns],
                    both[:, slot * rank : (slot + 1) * rank],
                ],
                axis=1,
            )
            out_upq[tenant] += upq_ref[j, slot * heads : (slot + 1) * heads]
            out_upkv[tenant] += upkv_ref[j, slot * 2 : (slot + 1) * 2]


def on_device(
    normed_input_rows,
    frozen_queries,
    frozen_keys,
    frozen_values,
    attention_output_gradient,
    adapter_down_weight,
    adapter_up_query,
    adapter_up_key_value,
    document_numbers,
    block_tenant_slot,
    shard_tenant_table,
    *,
    n_dp,
    n_mp,
):
    row_total = normed_input_rows.shape[0]
    tenants, columns, three_rank = adapter_down_weight.shape
    heads = frozen_queries.shape[1] // LANES
    upq = adapter_up_query.reshape(tenants, heads, LANES)
    upkv = adapter_up_key_value.reshape(tenants, 2, LANES)
    slots = jnp.broadcast_to(
        jnp.repeat(block_tenant_slot.astype(F32), row_total // block_tenant_slot.shape[0])[:, None],
        (row_total, LANES),
    )
    down_shape = (n_dp, 3 * columns, LANES)
    upq_shape = (n_dp, 2 * heads, LANES)
    upkv_shape = (n_dp, 4, LANES)
    packed = row_total * three_rank // LANES
    vmem = pl.BlockSpec(memory_space=pltpu.VMEM)
    smem = pl.BlockSpec(memory_space=pltpu.SMEM)
    sums = [
        pltpu.VMEM((packed, LANES), F32),
        pltpu.VMEM((n_mp, packed // n_mp, LANES), F32),
        pltpu.VMEM((packed, LANES), F32),
    ]
    got = pl.pallas_call(
        functools.partial(whole_kernel, n_dp, n_mp),
        out_shape=[jax.ShapeDtypeStruct(s, F32) for s in (down_shape, upq_shape, upkv_shape)],
        in_specs=[vmem] * 11 + [smem],
        out_specs=[vmem] * 3,
        scratch_shapes=[
            pltpu.VMEM(down_shape, F32),
            pltpu.VMEM(upq_shape, F32),
            pltpu.VMEM(upkv_shape, F32),
            pltpu.VMEM(down_shape, F32),
            pltpu.VMEM(upq_shape, F32),
            pltpu.VMEM(upkv_shape, F32),
            *sums,
            *sums,
            pltpu.VMEM((row_total, row_total), F32),
            pltpu.VMEM(upq_shape, F32),
            pltpu.VMEM(upkv_shape, F32),
            pltpu.VMEM(down_shape, F32),
            pltpu.SemaphoreType.DMA((12, n_dp)),
            pltpu.SemaphoreType.DMA((2, 4, n_mp)),
        ],
        compiler_params=pltpu.CompilerParams(
            collective_id=0, has_side_effects=True, vmem_limit_bytes=60 * 1024 * 1024
        ),
        name="whole",
    )(
        normed_input_rows,
        frozen_queries,
        frozen_keys,
        frozen_values,
        attention_output_gradient,
        adapter_down_weight,
        upq,
        upkv,
        slots,
        document_numbers[:, None],
        document_numbers[None, :],
        shard_tenant_table,
    )
    grad_down, grad_upq, grad_upkv = pl.pallas_call(
        owner_kernel,
        out_shape=[
            jax.ShapeDtypeStruct(adapter_down_weight.shape, F32),
            jax.ShapeDtypeStruct(upq.shape, F32),
            jax.ShapeDtypeStruct(upkv.shape, F32),
        ],
        in_specs=[vmem] * 3 + [smem],
        out_specs=[vmem] * 3,
        name="owner",
    )(*got, shard_tenant_table)
    return (
        grad_down,
        grad_upq.reshape(adapter_up_query.shape),
        grad_upkv.reshape(adapter_up_key_value.shape),
    )


def solution(mesh):
    placed = (
        P("dp", "mp"),
        P("dp", "mp"),
        P("dp", "mp"),
        P("dp", "mp"),
        P("dp", "mp"),
        P(None, ("mp", "dp"), None),
        P(None, "dp", "mp"),
        P(None, "dp", "mp", None),
        P("dp"),
        P("dp"),
        P(),
    )
    return jax.shard_map(
        functools.partial(on_device, n_dp=mesh.shape["dp"], n_mp=mesh.shape["mp"]),
        mesh=mesh,
        in_specs=placed,
        out_specs=(P(None, ("mp", "dp"), None), P(None, "dp", "mp"), P(None, "dp", "mp", None)),
        check_vma=False,
    )
```

time: 656 us -> 256 us (0.39)
  waiting for transfers between devices: 291 us -> 0 us
  Pallas kernels: 0 us -> 249 us
  blocking collectives: 192 us -> 0 us
  starting transfers between devices: 79.2 us -> 0 us
  local copies, waits for them, and re-layouts: 42.8 us -> 4.95 us
  matrix products: 29.8 us -> 0 us
  between operations: 15.3 us -> 0.64 us
    pallas_call x0 -> x2, Pallas kernels: none -> 249 us  [the longest x1 242 us: on_device(): pl.pallas_call(functools.partial(whole_kernel, n_dp, n_mp), out_shape=[ja...]
    unnamed x1 -> x0, blocking collectives: 192 us -> none
    all_to_all x6 -> x0, waiting for transfers between devices: 147 us -> none  [the longest x1 96.2 us: on_device(): lax.all_to_all(adapter_down_weight[desired_result], 'dp', split_axis=0, c...]
    psum x2 -> x0, waiting for transfers between devices: 143 us -> none  [the longest x1 83.9 us: on_device(): lax.psum(gradient_portion.reshape(row_count, 3 * adapter_rank), 'mp')]
    all_to_all x6 -> x0, starting transfers between devices: 78.9 us -> none  [the longest x1 20.8 us: on_device(): lax.all_to_all(down_terms, 'dp', split_axis=1, concat_axis=0, tiled=True)]
    dot_general x19 -> x0, matrix products: 29.8 us -> none  [the longest x3 5.1 us: adapted(): jnp.einsum('brk,bkc->brc', low_part, panel_cols, precision=PRECISION_HIGH)]
    gather x9 -> x0, local copies, waits for them, and re-layouts: 11.3 us -> none  [the longest x1 2.22 us: on_device(): owners = shard_tenant_table[senders, all_slots]]
    all_to_all x8 -> x0, local copies, waits for them, and re-layouts: 8.91 us -> none  [the longest x2 3.51 us: on_device(): lax.all_to_all(adapter_down_weight[desired_result], 'dp', split_axis=0, c...]
  transfers between devices with their start and end apart: 8 -> 0, of which waited for: 6 -> 0; matrix products, arithmetic and copies ran while one was open for 7% -> 0% of each run, Pallas kernels for 0% -> 0%
where the time goes in v1:
time: 256 us; the launch traced here: 255 us
  Pallas kernels  249 us (97%)
  local copies, waits for them, and re-layouts  4.95 us (2%)
    pallas_call x1, Pallas kernels, on_device(): pl.pallas_call(functools.partial(whole_kernel, n_dp, n_mp), out_shape=[ja...  242 us
    pallas_call x1, Pallas kernels, on_device(): pl.pallas_call(owner_kernel, out_shape=[jax.ShapeDtypeStruct(adapter_down...  7.29 us

profile of v1, /device:TPU:1, one launch (start us, length us, event | category | flops | bytes accessed | tf_op | source)
XLA Modules:
  0.0 255.4 jit_solution(8741474583058498181)
XLA Ops:
  0.6 0.7 convert_element_type.3
  1.3 0.1 broadcast_bitcast_fusion
  1.4 1.2 broadcast_in_dim.20.doc_row_ref
  2.6 1.4 copy.19.table_ref
  4.0 0.8 broadcast_in_dim.18.slot_ref
  4.8 1.5 broadcast_in_dim.21.doc_col_ref
  6.2 241.8 %whole.1 = (f32[64,48,128]{2,1,0:T(8,128)}, f32[64,16,128]{2,1,0:T(8,128)}, f32[64,4,128]{2,1,0:T(4,128)}) custom-call(bf16[384,1024]{1,0:T(8,128)(2,1)} %rows_ref.1, bf16[384,1024]{1,0:T(8,128)(2,1)} %queries_ref.1, bf16[384,128]{1,0:T(8,128)(2,1)} %keys_ref.1, bf16[384,128]{1,0:T(8,128)(2,1)} %values_ref.1, bf16[384,1024]{1,0:T(8,128)(2,1)} %upstream_ref.1, ...), custom_call_target="tpu_custom_call" | custom-call | tf_op jit(solution)/shard_map/whole/pallas_call | solution.py:433
  248.1 7.3 %owner.1 = (f32[64,16,192]{2,1,0:T(8,128)}, f32[64,8,128]{2,1,0:T(8,128)}, f32[64,2,128]{2,1,0:T(2,128)}) custom-call(f32[64,48,128]{2,1,0:T(8,128)} %get-tuple-element.9.down_ref, f32[64,16,128]{2,1,0:T(8,128)} %get-tuple-element.10.upq_ref, f32[64,4,128]{2,1,0:T(4,128)} %get-tuple-element.11.upkv_ref, s32[64,2]{1,0:T(8,128)} %copy.19.table_ref), custom_call_target="tpu_custom_call" | custom-call | tf_op jit(solution)/shard_map/owner/pallas_call | solution.py:472

commit v2 on v1

v2 whole, which is shorter than its diff:
```python
import functools

import jax
import jax.numpy as jnp
from jax import lax
from jax.experimental import pallas as pl
from jax.experimental.pallas import tpu as pltpu
from jax.sharding import PartitionSpec as P

ADAPTER_SCALE = 0.5
MASKED = -1e30
MESH = pl.DeviceIdType.MESH
LANES = 128
DOC_ROWS = 16
F32 = jnp.float32
BF16 = jnp.bfloat16


def dot(a, b, ca, cb):
    return lax.dot_general(a, b, (((ca,), (cb,)), ((), ())), preferred_element_type=F32)


def parts(a):
    high = a.astype(BF16)
    return high, (a - high.astype(F32)).astype(BF16)


def dot_exact_left(a, b, ca, cb):
    high, low = parts(b)
    return dot(a, high, ca, cb) + dot(a, low, ca, cb)


def dot_both(a, b, ca, cb):
    a_high, a_low = parts(a)
    b_high, b_low = parts(b)
    return dot(a_high, b_high, ca, cb) + (dot(a_high, b_low, ca, cb) + dot(a_low, b_high, ca, cb))


def barrier(dp, mp, n_dp, n_mp):
    sem = pltpu.get_barrier_semaphore()

    @pl.loop(1, n_dp)
    def _(k):
        pl.semaphore_signal(
            sem, inc=1, device_id={"dp": lax.rem(dp + k, n_dp)}, device_id_type=MESH
        )

    for k in range(1, n_mp):
        pl.semaphore_signal(
            sem, inc=1, device_id={"mp": lax.rem(mp + k, n_mp)}, device_id_type=MESH
        )
    return lambda: pl.semaphore_wait(sem, n_dp - 1 + n_mp - 1)


class Exchange:
    def __init__(self, source, target, send, recv, dp, n_dp):
        self.source, self.target, self.send, self.recv = source, target, send, recv
        self.dp, self.n_dp = dp, n_dp

    def piece(self, k, peer, slot):
        return pltpu.make_async_remote_copy(
            src_ref=self.source.at[peer],
            dst_ref=self.target.at[slot],
            send_sem=self.send.at[k],
            recv_sem=self.recv.at[k],
            device_id={"dp": peer},
            device_id_type=MESH,
        )

    def start(self, k):
        self.piece(k, lax.rem(self.dp + k, self.n_dp), self.dp).start()

    def keep(self):
        self.target[pl.ds(self.dp, 1)] = self.source[pl.ds(self.dp, 1)]

    def wait_recv(self):
        @pl.loop(1, self.n_dp)
        def _(k):
            origin = lax.rem(self.dp + self.n_dp - k, self.n_dp)
            self.piece(k, origin, origin).wait_recv()

    def wait_send(self):
        @pl.loop(1, self.n_dp)
        def _(k):
            self.piece(k, lax.rem(self.dp + k, self.n_dp), self.dp).wait_send()


def start_all(exchanges, n_dp):
    for group in exchanges:

        @pl.loop(0, n_dp - 1)
        def _(i):
            half = lax.div(i + 2, 2)
            k = jnp.where(lax.rem(i, 2) == 0, half, n_dp - half)
            for exchange in group:
                exchange.start(k)


class SumOverMp:
    def __init__(self, partial, landed, total, sems, mp, n_mp):
        self.partial, self.landed, self.total = partial, landed, total
        self.mp, self.n_mp = mp, n_mp
        self.rows = partial.shape[0] // n_mp
        self.sems = sems

    def rows_of(self, p):
        return pl.ds(pl.multiple_of(p * self.rows, 8), self.rows)

    def copy(self, k, second):
        peer = lax.rem(self.mp + k, self.n_mp)
        if second:
            source = target = self.total.at[self.rows_of(self.mp)]
        else:
            source, target = self.partial.at[self.rows_of(peer)], self.landed.at[k]
        return pltpu.make_async_remote_copy(
            src_ref=source,
            dst_ref=target,
            send_sem=self.sems.at[2 * second, k],
            recv_sem=self.sems.at[2 * second + 1, k],
            device_id={"mp": peer},
            device_id_type=MESH,
        )

    def landed_total(self, k):
        origin = lax.rem(self.mp + self.n_mp - k, self.n_mp)
        return pltpu.make_async_remote_copy(
            src_ref=self.total.at[self.rows_of(origin)],
            dst_ref=self.total.at[self.rows_of(origin)],
            send_sem=self.sems.at[2, k],
            recv_sem=self.sems.at[3, k],
            device_id={"mp": origin},
            device_id_type=MESH,
        )

    def scatter(self):
        for k in range(1, self.n_mp):
            self.copy(k, 0).start()

    def gather(self):
        mine = self.partial[self.rows_of(self.mp)]
        for k in range(1, self.n_mp):
            self.copy(k, 0).wait_recv()
            mine = mine + self.landed[k]
        self.total[self.rows_of(self.mp)] = mine
        for k in range(1, self.n_mp):
            self.copy(k, 1).start()

    def arrive(self):
        for k in range(1, self.n_mp):
            self.landed_total(k).wait_recv()

    def finish(self):
        for k in range(1, self.n_mp):
            self.copy(k, 0).wait_send()
            self.copy(k, 1).wait_send()


def store_packed(ref, wide, narrow):
    rows = wide.shape[0]
    half = rows // 2
    ref[0:rows] = wide
    ref[rows : rows + half] = jnp.concatenate([narrow[0:half], narrow[half:rows]], axis=1)


def load_packed(ref, rows):
    half = rows // 2
    tail = ref[rows : rows + half]
    width = tail.shape[1] // 2
    return ref[0:rows], jnp.concatenate([tail[:, :width], tail[:, width:]], axis=0)


def whole_kernel(
    n_dp,
    n_mp,
    groups,
    rows_hbm,
    queries_hbm,
    keys_hbm,
    values_hbm,
    upstream_hbm,
    down_hbm,
    upq_hbm,
    upkv_hbm,
    slot_ref,
    doc_ref,
    table_ref,
    got_down_ref,
    got_upq_ref,
    got_upkv_ref,
    rows_ref,
    queries_ref,
    keys_ref,
    values_ref,
    upstream_ref,
    down_ref,
    upq_ref,
    upkv_ref,
    send_down,
    send_upq,
    send_upkv,
    recv_down,
    recv_upq,
    recv_upkv,
    partial,
    landed,
    total,
    partial_back,
    landed_back,
    total_back,
    rows_turned,
    bias,
    grad_query_turned,
    grad_key,
    grad_value,
    send_upq_back,
    send_upkv_back,
    send_down_back,
    load_sems,
    exchange_sems,
    sum_sems,
):
    dp, mp = lax.axis_index("dp"), lax.axis_index("mp")
    row_total = rows_ref.shape[0]
    rank = down_ref.shape[2] // 3
    wide = 2 * rank
    columns = down_ref.shape[1]
    heads = queries_ref.shape[1] // LANES
    per_group = heads // groups
    group_lanes = per_group * LANES
    blocks = slot_ref.shape[0]
    block_rows = row_total // blocks
    inverse = 1.0 / float(LANES) ** 0.5

    loads = [
        pltpu.make_async_copy(source, target, load_sems.at[i])
        for i, (source, target) in enumerate(
            [
                (down_hbm, down_ref),
                (upq_hbm, upq_ref),
                (upkv_hbm, upkv_ref),
                (rows_hbm, rows_ref),
                (keys_hbm, keys_ref),
                (values_hbm, values_ref),
                (queries_hbm, queries_ref),
                (upstream_hbm, upstream_ref),
            ]
        )
    ]
    for load in loads:
        load.start()
    arrived = barrier(dp, mp, n_dp, n_mp)
    for load in loads[:3]:
        load.wait()

    @pl.loop(0, n_dp)
    def _(d):
        first, second = table_ref[0, d], table_ref[1, d]
        a, b = down_ref[first], down_ref[second]
        send_down[d] = jnp.concatenate(
            [a[:, :wide], b[:, :wide], jnp.concatenate([a[:, wide:], b[:, wide:]], axis=1)],
            axis=0,
        )
        a, b = upq_ref[first], upq_ref[second]
        for g in range(groups):
            span = slice(g * per_group, (g + 1) * per_group)
            send_upq[g, d] = jnp.concatenate([a[span], b[span]], axis=0)
        send_upkv[d, 0:2] = upkv_ref[first]
        send_upkv[d, 2:4] = upkv_ref[second]

    arrived()

    def exchange(index, source, target):
        return Exchange(
            source, target, exchange_sems.at[2 * index], exchange_sems.at[2 * index + 1], dp, n_dp
        )

    down_in = exchange(0, send_down, recv_down)
    upkv_in = exchange(1, send_upkv, recv_upkv)
    upq_in = [exchange(2 + g, send_upq.at[g], recv_upq.at[g]) for g in range(groups)]
    upkv_back = exchange(2 + groups, send_upkv_back, got_upkv_ref)
    down_back = exchange(3 + groups, send_down_back, got_down_ref)
    upq_back = [
        exchange(4 + groups + g, send_upq_back.at[g], got_upq_ref.at[g]) for g in range(groups)
    ]
    start_all([[down_in], [upkv_in, upq_in[0]]] + [[one] for one in upq_in[1:]], n_dp)
    for one in [down_in, upkv_in] + upq_in:
        one.keep()

    lane = lax.broadcasted_iota(jnp.int32, (1, row_total), 1)
    doc_lane = jnp.zeros((1, row_total), jnp.int32)
    for start in range(0, row_total, DOC_ROWS):
        doc_lane = jnp.where(lane >= start, doc_ref[start], doc_lane)
    sub = lax.broadcasted_iota(jnp.int32, (DOC_ROWS, row_total), 0)
    for start in range(0, row_total, DOC_ROWS):
        joined = (doc_lane == doc_ref[start]) & (sub + start <= lane)
        bias[start : start + DOC_ROWS] = jnp.where(joined, 0.0, MASKED).astype(F32)
    in_second = jnp.concatenate(
        [jnp.full((block_rows, LANES), slot_ref[b].astype(F32)) for b in range(blocks)], axis=0
    )
    in_first = 1.0 - in_second
    for load in loads[3:]:
        load.wait()
    rows = rows_ref[...]
    rows_turned[...] = rows.T

    down_in.wait_recv()
    panels = jnp.concatenate(
        [
            recv_down[:, i * columns : (i + 1) * columns, :].reshape(n_dp * columns, LANES)
            for i in range(3)
        ],
        axis=1,
    )
    low = dot(rows, jnp.concatenate(parts(panels), axis=1), 1, 0)
    low = low[:, : 3 * LANES] + low[:, 3 * LANES :]
    low_wide = low[:, :LANES] * in_first + low[:, LANES : 2 * LANES] * in_second
    both = low[:, 2 * LANES :]
    low_narrow = both[:, :rank] * in_first[:, :rank] + both[:, rank:] * in_second[:, :rank]
    store_packed(partial, low_wide, low_narrow)
    low_sum = SumOverMp(partial, landed, total, sum_sems.at[0], mp, n_mp)
    low_sum.scatter()
    low_sum.gather()
    low_sum.arrive()
    low_wide, low_v = load_packed(total, row_total)

    def by_slot(low):
        return jnp.concatenate(
            [low * in_first[:, :rank], low * in_second[:, :rank]], axis=1
        )

    low_q = by_slot(low_wide[:, :rank])
    low_k = by_slot(low_wide[:, rank:])
    low_v = by_slot(low_v)

    def adapted(frozen, low, panel):
        return (frozen.astype(F32) + ADAPTER_SCALE * dot_both(low, panel, 1, 0)).astype(BF16)

    upkv_in.wait_recv()
    up_k = jnp.concatenate([recv_upkv[:, 0, :], recv_upkv[:, 2, :]], axis=0)
    up_v = jnp.concatenate([recv_upkv[:, 1, :], recv_upkv[:, 3, :]], axis=0)
    key = adapted(keys_ref[...], low_k, up_k)
    value = adapted(values_ref[...], low_v, up_v)
    key_turned = key.T
    grad_key[...] = jnp.zeros_like(grad_key)
    grad_value[...] = jnp.zeros_like(grad_value)
    grad_low_q = jnp.zeros((wide, row_total), F32)
    for g in range(groups):
        lanes = slice(g * group_lanes, (g + 1) * group_lanes)
        upq_in[g].wait_recv()
        panel = jnp.concatenate(
            [
                jnp.concatenate(
                    [recv_upq[g, :, h, :], recv_upq[g, :, per_group + h, :]], axis=0
                )
                for h in range(per_group)
            ],
            axis=1,
        )
        query = adapted(queries_ref[:, lanes], low_q, panel)
        upstream = upstream_ref[:, lanes]

        def stacked(a, first):
            return jnp.concatenate(
                [
                    a[first : first + block_rows, h * LANES : (h + 1) * LANES]
                    for h in range(per_group)
                ],
                axis=0,
            )

        for b in range(blocks):
            first, last = b * block_rows, (b + 1) * block_rows
            query_b, upstream_b = stacked(query, first), stacked(upstream, first)
            mask = jnp.concatenate([bias[0:last, first:last]] * per_group, axis=1)
            scores = dot(key[:last], query_b, 1, 1) * inverse + mask
            weights = jnp.exp(scores - jnp.max(scores, axis=0, keepdims=True))
            probs = weights * (1.0 / jnp.sum(weights, axis=0, keepdims=True))
            grad_probs = dot(value[:last], upstream_b, 1, 1)
            inner = jnp.sum(probs * grad_probs, axis=0, keepdims=True)
            grad_scores = (probs * (grad_probs - inner) * inverse).astype(BF16)
            grad_key[0:last] += dot(grad_scores, query_b, 1, 0)
            grad_value[0:last] += dot(probs.astype(BF16), upstream_b, 1, 0)
            turned = dot(key_turned[:, :last], grad_scores, 1, 0)
            for h in range(per_group):
                grad_query_turned[h * LANES : (h + 1) * LANES, first:last] = turned[
                    :, h * block_rows : (h + 1) * block_rows
                ]
        grad_query = grad_query_turned[...]
        term = ADAPTER_SCALE * dot_both(grad_query, low_q, 1, 0)
        for h in range(per_group):
            turned = term[h * LANES : (h + 1) * LANES].T
            send_upq_back[g, :, h, :] = turned[:rank]
            send_upq_back[g, :, per_group + h, :] = turned[rank:]
        grad_low_q = grad_low_q + dot_both(panel, grad_query, 1, 0)
        if g < groups - 1:
            start_all([[upq_back[g]]], n_dp)

    def of_slot(grad):
        return ADAPTER_SCALE * (
            grad[:, :rank] * in_first[:, :rank] + grad[:, rank:] * in_second[:, :rank]
        )

    grad_k, grad_v = grad_key[...], grad_value[...]
    store_packed(
        partial_back,
        jnp.concatenate(
            [of_slot(grad_low_q.T), of_slot(dot_both(grad_k, up_k, 1, 1))], axis=1
        ),
        of_slot(dot_both(grad_v, up_v, 1, 1)),
    )
    grad_sum = SumOverMp(partial_back, landed_back, total_back, sum_sems.at[1], mp, n_mp)
    term = ADAPTER_SCALE * dot_both(low_k, grad_k, 0, 0)
    send_upkv_back[:, 0, :] = term[:rank]
    send_upkv_back[:, 2, :] = term[rank:]
    term = ADAPTER_SCALE * dot_both(low_v, grad_v, 0, 0)
    send_upkv_back[:, 1, :] = term[:rank]
    send_upkv_back[:, 3, :] = term[rank:]
    grad_sum.scatter()
    start_all([[upq_back[groups - 1], upkv_back]], n_dp)
    grad_sum.gather()
    for one in [upkv_back] + upq_back:
        one.keep()
    grad_sum.arrive()
    grad_wide, grad_narrow = load_packed(total_back, row_total)
    grads = jnp.concatenate(
        [
            grad_wide * in_first,
            grad_wide * in_second,
            grad_narrow * in_first[:, :rank],
            grad_narrow * in_second[:, :rank],
        ],
        axis=1,
    )
    term = dot(rows_turned[...], jnp.concatenate(parts(grads), axis=1), 1, 0)
    for i in range(3):
        send_down_back[:, i * columns : (i + 1) * columns, :] = (
            term[:, i * LANES : (i + 1) * LANES] + term[:, (3 + i) * LANES : (4 + i) * LANES]
        ).reshape(n_dp, columns, LANES)
    start_all([[down_back]], n_dp)
    down_back.keep()

    for one in [down_in, upkv_in] + upq_in:
        one.wait_send()
    low_sum.finish()
    grad_sum.finish()
    for one in [upkv_back] + upq_back + [down_back]:
        one.wait_recv()
        one.wait_send()


def owner_kernel(down_ref, upq_ref, upkv_ref, table_ref, out_down, out_upq, out_upkv):
    tenants, columns = out_down.shape[0], out_down.shape[1]
    rank = out_down.shape[2] // 3
    groups, n_dp = upq_ref.shape[0], upq_ref.shape[1]
    per_group = upq_ref.shape[2] // 2
    tenant = lax.broadcasted_iota(jnp.int32, (tenants, n_dp), 0)
    owned = [
        jnp.where(tenant == table_ref[slot : slot + 1, :], 1.0, 0.0).astype(BF16)
        for slot in range(2)
    ]
    owned_both = jnp.concatenate(owned, axis=1)

    def owner_sum(pairs):
        terms = jnp.concatenate(
            [jnp.concatenate([a, b], axis=0) for a, b in pairs], axis=1
        )
        return dot_exact_left(owned_both, terms, 1, 0)

    def spread(ref, first, count, step, store):
        for start in range(0, count, 4):
            span = range(start, min(start + 4, count))
            total = owner_sum([(ref[:, first + r, :], ref[:, first + step + r, :]) for r in span])
            for n, r in enumerate(span):
                store(r, total[:, n * LANES : (n + 1) * LANES])

    def store_down(r, total):
        out_down[:, r, 0:LANES] = total

    spread(down_ref, 0, columns, columns, store_down)
    for start in range(0, columns, 4):
        both = jnp.concatenate(
            [down_ref[:, 2 * columns + r, :] for r in range(start, start + 4)], axis=1
        )
        of_first = dot_exact_left(owned[0], both, 1, 0)
        of_second = dot_exact_left(owned[1], both, 1, 0)
        for n in range(4):
            out_down[:, start + n, LANES : LANES + rank] = (
                of_first[:, n * LANES : n * LANES + rank]
                + of_second[:, n * LANES + rank : (n + 1) * LANES]
            )
    for g in range(groups):

        def store_upq(r, total, g=g):
            out_upq[:, g * per_group + r, :] = total

        spread(upq_ref.at[g], 0, per_group, per_group, store_upq)

    def store_upkv(r, total):
        out_upkv[:, r, :] = total

    spread(upkv_ref, 0, 2, 2, store_upkv)


def on_device(
    normed_input_rows,
    frozen_queries,
    frozen_keys,
    frozen_values,
    attention_output_gradient,
    adapter_down_weight,
    adapter_up_query,
    adapter_up_key_value,
    document_numbers,
    block_tenant_slot,
    shard_tenant_table,
    *,
    n_dp,
    n_mp,
):
    row_total = normed_input_rows.shape[0]
    tenants, columns, three_rank = adapter_down_weight.shape
    heads = frozen_queries.shape[1] // LANES
    upq = adapter_up_query.reshape(tenants, heads, LANES)
    upkv = adapter_up_key_value.reshape(tenants, 2, LANES)
    groups = 2
    table = shard_tenant_table.T
    down_shape = (n_dp, 3 * columns, LANES)
    upq_shape = (groups, n_dp, 2 * heads // groups, LANES)
    upkv_shape = (n_dp, 4, LANES)
    packed = row_total * three_rank // LANES
    vmem = pl.BlockSpec(memory_space=pltpu.VMEM)
    smem = pl.BlockSpec(memory_space=pltpu.SMEM)
    sums = [
        pltpu.VMEM((packed, LANES), F32),
        pltpu.VMEM((n_mp, packed // n_mp, LANES), F32),
        pltpu.VMEM((packed, LANES), F32),
    ]
    loaded = (
        normed_input_rows,
        frozen_queries,
        frozen_keys,
        frozen_values,
        attention_output_gradient,
        adapter_down_weight,
        upq,
        upkv,
    )
    got = pl.pallas_call(
        functools.partial(whole_kernel, n_dp, n_mp, groups),
        out_shape=[jax.ShapeDtypeStruct(s, F32) for s in (down_shape, upq_shape, upkv_shape)],
        in_specs=[pl.BlockSpec(memory_space=pl.ANY)] * 8 + [smem] * 3,
        out_specs=[vmem] * 3,
        scratch_shapes=[
            *(pltpu.VMEM(a.shape, a.dtype) for a in loaded),
            pltpu.VMEM(down_shape, F32),
            pltpu.VMEM(upq_shape, F32),
            pltpu.VMEM(upkv_shape, F32),
            pltpu.VMEM(down_shape, F32),
            pltpu.VMEM(upq_shape, F32),
            pltpu.VMEM(upkv_shape, F32),
            *sums,
            *sums,
            pltpu.VMEM(normed_input_rows.shape[::-1], BF16),
            pltpu.VMEM((row_total, row_total), F32),
            pltpu.VMEM((heads // groups * LANES, row_total), F32),
            pltpu.VMEM((row_total, LANES), F32),
            pltpu.VMEM((row_total, LANES), F32),
            pltpu.VMEM(upq_shape, F32),
            pltpu.VMEM(upkv_shape, F32),
            pltpu.VMEM(down_shape, F32),
            pltpu.SemaphoreType.DMA((len(loaded),)),
            pltpu.SemaphoreType.DMA((8 + 4 * groups, n_dp)),
            pltpu.SemaphoreType.DMA((2, 4, n_mp)),
        ],
        compiler_params=pltpu.CompilerParams(
            collective_id=0, has_side_effects=True, vmem_limit_bytes=60 * 1024 * 1024
        ),
        name="whole",
    )(*loaded, block_tenant_slot, document_numbers, table)
    grad_down, grad_upq, grad_upkv = pl.pallas_call(
        owner_kernel,
        out_shape=[
            jax.ShapeDtypeStruct(adapter_down_weight.shape, F32),
            jax.ShapeDtypeStruct(upq.shape, F32),
            jax.ShapeDtypeStruct(upkv.shape, F32),
        ],
        in_specs=[vmem] * 4,
        out_specs=[vmem] * 3,
        name="owner",
    )(*got, table)
    return (
        grad_down,
        grad_upq.reshape(adapter_up_query.shape),
        grad_upkv.reshape(adapter_up_key_value.shape),
    )


def solution(mesh):
    placed = (
        P("dp", "mp"),
        P("dp", "mp"),
        P("dp", "mp"),
        P("dp", "mp"),
        P("dp", "mp"),
        P(None, ("mp", "dp"), None),
        P(None, "dp", "mp"),
        P(None, "dp", "mp", None),
        P("dp"),
        P("dp"),
        P(),
    )
    return jax.shard_map(
        functools.partial(on_device, n_dp=mesh.shape["dp"], n_mp=mesh.shape["mp"]),
        mesh=mesh,
        in_specs=placed,
        out_specs=(P(None, ("mp", "dp"), None), P(None, "dp", "mp"), P(None, "dp", "mp", None)),
        check_vma=False,
    )
```

time: 256 us -> 232 us (0.906)
  Pallas kernels: 249 us -> 230 us
  local copies, waits for them, and re-layouts: 4.95 us -> 0 us
    pallas_call x1, Pallas kernels: 242 us -> 226 us  [on_device(): pl.pallas_call(functools.partial(whole_kernel, n_dp, n_mp, groups), out_s...]
    broadcast_in_dim x4 -> x0, local copies, waits for them, and re-layouts: 3.58 us -> none  [the longest x1 1.47 us: on_device(): document_numbers[:, None]]
where the time goes in v2:
time: 232 us; the launch traced here: 231 us
  Pallas kernels  230 us (99%)
    pallas_call x1, Pallas kernels, on_device(): pl.pallas_call(functools.partial(whole_kernel, n_dp, n_mp, groups), out_s...  226 us
    pallas_call x1, Pallas kernels, on_device(): pl.pallas_call(owner_kernel, out_shape=[jax.ShapeDtypeStruct(adapter_down...  4.89 us

profile of v2, /device:TPU:1, one launch (start us, length us, event | category | flops | bytes accessed | tf_op | source)
XLA Modules:
  0.0 231.1 jit_solution(13632641798253034190)
XLA Ops:
  0.6 225.6 %whole.1 = (f32[64,48,128]{2,1,0:T(8,128)}, f32[2,64,8,128]{3,2,1,0:T(8,128)}, f32[64,4,128]{2,1,0:T(4,128)}) custom-call(bf16[384,1024]{1,0:T(8,128)(2,1)} %rows_hbm.1, bf16[384,1024]{1,0:T(8,128)(2,1)} %queries_hbm.1, bf16[384,128]{1,0:T(8,128)(2,1)} %keys_hbm.1, bf16[384,128]{1,0:T(8,128)(2,1)} %values_hbm.1, bf16[384,1024]{1,0:T(8,128)(2,1)} %upstream_hbm.1, ...), custom_call_target="tpu_custom_call" | custom-call | tf_op jit(solution)/shard_map/whole/pallas_call | solution.py:548
  226.2 4.9 %owner.1 = (f32[64,16,192]{2,1,0:T(8,128)}, f32[64,8,128]{2,1,0:T(8,128)}, f32[64,2,128]{2,1,0:T(2,128)}) custom-call(f32[64,48,128]{2,1,0:T(8,128)} %get-tuple-element.9.down_ref, f32[2,64,8,128]{3,2,1,0:T(8,128)} %get-tuple-element.10.upq_ref, f32[64,4,128]{2,1,0:T(4,128)} %get-tuple-element.11.upkv_ref, s32[2,64]{1,0:T(2,128)} %bitcast.8), custom_call_target="tpu_custom_call" | custom-call | tf_op jit(solution)/shard_map/owner/pallas_call | solution.py:580

commit v3 on v2

v3 whole, which is shorter than its diff:
```python
import functools

import jax
import jax.numpy as jnp
from jax import lax
from jax.experimental import pallas as pl
from jax.experimental.pallas import tpu as pltpu
from jax.sharding import PartitionSpec as P

ADAPTER_SCALE = 0.5
MASKED = -1e30
MESH = pl.DeviceIdType.MESH
LANES = 128
DOC_ROWS = 16
PLANE = 4
F32 = jnp.float32
BF16 = jnp.bfloat16


def dot(a, b, ca, cb):
    return lax.dot_general(a, b, (((ca,), (cb,)), ((), ())), preferred_element_type=F32)


def parts(a):
    high = a.astype(BF16)
    return high, (a - high.astype(F32)).astype(BF16)


def dot_exact_left(a, b, ca, cb):
    high, low = parts(b)
    return dot(a, high, ca, cb) + dot(a, low, ca, cb)


def dot_both(a, b, ca, cb):
    a_high, a_low = parts(a)
    b_high, b_low = parts(b)
    return dot(a_high, b_high, ca, cb) + (dot(a_high, b_low, ca, cb) + dot(a_low, b_high, ca, cb))


def signal(sem, **device):
    pl.semaphore_signal(sem, inc=1, device_id=device, device_id_type=MESH)


class Place:
    def __init__(self, n_dp, n_mp):
        self.n_dp, self.n_mp = n_dp, n_mp
        self.planes = n_dp // PLANE
        self.per = self.planes // n_mp
        self.dp, self.mp = lax.axis_index("dp"), lax.axis_index("mp")
        self.z, self.q = lax.div(self.dp, PLANE), lax.rem(self.dp, PLANE)
        self.worker_slot = lax.div(self.z, n_mp)
        self.is_own_worker = self.worker_mp(self.z) == self.mp

    def worker_mp(self, z):
        return lax.rem(self.z + z, self.n_mp)

    def worker(self, dz):
        z = lax.rem(self.z + dz, self.planes)
        return z, {"dp": z * PLANE + self.q, "mp": self.worker_mp(z)}

    def served_z(self, w, m):
        return lax.rem(m + self.planes - self.z, self.n_mp) + w * self.n_mp

    def served(self, w, m=None, q=None):
        m, q = (self.mp, self.q) if m is None else (m, q)
        return self.served_z(w, m) * PLANE + q

    def serves_own_plane(self, w):
        return self.served_z(w, self.mp) == self.z

    def mate(self, k, sign):
        dq, dm = lax.div(k, self.n_mp), lax.rem(k, self.n_mp)
        q = lax.rem(self.q + PLANE + sign * dq, PLANE)
        m = lax.rem(self.mp + self.n_mp + sign * dm, self.n_mp)
        return q, m


def barrier(at):
    sem = pltpu.get_barrier_semaphore()

    @pl.loop(1, at.n_dp)
    def _(k):
        signal(sem, dp=lax.rem(at.dp + k, at.n_dp))

    for k in range(1, at.n_mp):
        signal(sem, mp=lax.rem(at.mp + k, at.n_mp))

    @pl.loop(at.n_mp, PLANE * at.n_mp)
    def _(k):
        q, m = at.mate(k, 1)

        @pl.when(m != at.mp)
        def _():
            signal(sem, dp=at.z * PLANE + q, mp=m)

    @pl.loop(1, at.planes)
    def _(dz):
        _, device = at.worker(dz)
        signal(sem, **device)

    for w in range(at.per):

        @pl.when(jnp.logical_not(at.serves_own_plane(w)))
        def _():
            @pl.loop(0, at.n_mp)
            def _(m):
                signal(sem, dp=at.served(w), mp=m)

    count = (at.n_dp - 1) + (at.n_mp - 1) + (PLANE - 1) * (at.n_mp - 1) + (at.planes - 1)
    count = count + at.n_mp * at.per - jnp.where(at.is_own_worker, at.n_mp, 0)
    return lambda: pl.semaphore_wait(sem, count)


def remote(source, target, send, recv, **device):
    return pltpu.make_async_remote_copy(
        src_ref=source,
        dst_ref=target,
        send_sem=send,
        recv_sem=recv,
        device_id=device,
        device_id_type=MESH,
    )


class ToWorkers:
    def __init__(self, at, source, target, send, recv, same):
        self.at, self.source, self.target, self.send, self.recv = at, source, target, send, recv
        self.same = same

    def copy(self, dz):
        z, device = self.at.worker(dz)
        source = self.source if self.same else self.source.at[z]
        slot = (self.at.worker_slot, self.at.mp)
        return remote(source, self.target.at[slot], self.send.at[dz], self.recv.at[slot], **device)

    def start(self):
        at = self.at

        @pl.loop(1, at.planes)
        def _(dz):
            self.copy(dz).start()

        @pl.when(jnp.logical_not(at.is_own_worker))
        def _():
            self.copy(0).start()

        @pl.when(at.is_own_worker)
        def _():
            self.target[at.worker_slot, at.mp] = (
                self.source[...] if self.same else self.source[at.z]
            )

    def wait_recv(self):
        at = self.at
        for w in range(at.per):

            @pl.loop(0, at.n_mp)
            def _(m):
                @pl.when(jnp.logical_not(at.serves_own_plane(w) & (m == at.mp)))
                def _():
                    place = self.target.at[w, m]
                    remote(
                        place, place, self.send.at[0], self.recv.at[w, m], dp=at.served(w), mp=m
                    ).wait_recv()

    def wait_send(self):
        @pl.loop(1, self.at.planes)
        def _(dz):
            self.copy(dz).wait_send()

        @pl.when(jnp.logical_not(self.at.is_own_worker))
        def _():
            self.copy(0).wait_send()


class FromWorkers:
    def __init__(self, at, source, target, send, recv):
        self.at, self.source, self.target, self.send, self.recv = at, source, target, send, recv

    def copy(self, w, m):
        at = self.at
        return remote(
            self.source.at[w, m],
            self.target.at[at.z],
            self.send.at[w, m],
            self.recv.at[at.z],
            dp=at.served(w),
            mp=m,
        )

    def each(self, act):
        at = self.at
        for w in range(at.per):

            @pl.loop(0, at.n_mp)
            def _(m):
                @pl.when(jnp.logical_not(at.serves_own_plane(w) & (m == at.mp)))
                def _():
                    act(self.copy(w, m))

    def start(self):
        at = self.at
        self.each(lambda copy: copy.start())

        @pl.when(at.is_own_worker)
        def _():
            self.target[at.z] = self.source[at.worker_slot, at.mp]

    def wait_recv(self):
        at = self.at

        @pl.loop(0, at.planes)
        def _(z):
            @pl.when(jnp.logical_not(at.is_own_worker & (z == at.z)))
            def _():
                place = self.target.at[z]
                remote(
                    place,
                    place,
                    self.send.at[0, 0],
                    self.recv.at[z],
                    dp=z * PLANE + at.q,
                    mp=at.worker_mp(z),
                ).wait_recv()

    def wait_send(self):
        self.each(lambda copy: copy.wait_send())


class InPlane:
    def __init__(self, at, pick, place, send, recv):
        self.at, self.pick, self.place, self.send, self.recv = at, pick, place, send, recv

    def copy(self, k, w, sign):
        at = self.at
        q, m = at.mate(k, sign)
        target = self.place(w, at.mp, at.q) if sign == 1 else self.place(w, m, q)
        source = self.pick(w, m, q) if sign == 1 else target
        return remote(
            source, target, self.send.at[k, w], self.recv.at[k, w], dp=at.z * PLANE + q, mp=m
        )

    def each(self, sign, act):
        @pl.loop(1, PLANE * self.at.n_mp)
        def _(k):
            for w in range(self.at.per):
                act(self.copy(k, w, sign))

    def start(self):
        self.each(1, lambda copy: copy.start())

    def keep(self):
        at = self.at
        for w in range(at.per):
            self.place(w, at.mp, at.q)[...] = self.pick(w, at.mp, at.q)[...]

    def wait_recv(self):
        self.each(-1, lambda copy: copy.wait_recv())

    def wait_send(self):
        self.each(1, lambda copy: copy.wait_send())


class Announce:
    def __init__(self, at, ref, send, recv):
        self.at, self.ref, self.send, self.recv = at, ref, send, recv

    def copy(self, k, sign):
        at = self.at
        peer = lax.rem(at.dp + at.n_dp + sign * k, at.n_dp)
        place = self.ref.at[at.dp if sign == 1 else peer]
        return remote(place, place, self.send.at[k], self.recv.at[k], dp=peer)

    def each(self, sign, act):
        @pl.loop(1, self.at.n_dp)
        def _(k):
            act(self.copy(k, sign))

    def start(self):
        self.each(1, lambda copy: copy.start())

    def wait_recv(self):
        self.each(-1, lambda copy: copy.wait_recv())

    def wait_send(self):
        self.each(1, lambda copy: copy.wait_send())


class Exchange:
    def __init__(self, source, target, send, recv, dp, n_dp):
        self.source, self.target, self.send, self.recv = source, target, send, recv
        self.dp, self.n_dp = dp, n_dp

    def piece(self, k, peer, slot):
        return pltpu.make_async_remote_copy(
            src_ref=self.source.at[peer],
            dst_ref=self.target.at[slot],
            send_sem=self.send.at[k],
            recv_sem=self.recv.at[k],
            device_id={"dp": peer},
            device_id_type=MESH,
        )

    def start(self, k):
        self.piece(k, lax.rem(self.dp + k, self.n_dp), self.dp).start()

    def keep(self):
        self.target[pl.ds(self.dp, 1)] = self.source[pl.ds(self.dp, 1)]

    def wait_recv(self):
        @pl.loop(1, self.n_dp)
        def _(k):
            origin = lax.rem(self.dp + self.n_dp - k, self.n_dp)
            self.piece(k, origin, origin).wait_recv()

    def wait_send(self):
        @pl.loop(1, self.n_dp)
        def _(k):
            self.piece(k, lax.rem(self.dp + k, self.n_dp), self.dp).wait_send()


def start_all(exchanges, n_dp):
    for group in exchanges:

        @pl.loop(0, n_dp - 1)
        def _(i):
            half = lax.div(i + 2, 2)
            k = jnp.where(lax.rem(i, 2) == 0, half, n_dp - half)
            for exchange in group:
                exchange.start(k)


class SumOverMp:
    def __init__(self, at, partial, landed, total, sems):
        self.at, self.partial, self.landed, self.total, self.sems = at, partial, landed, total, sems

    def scatter_copy(self, k):
        peer = lax.rem(self.at.mp + k, self.at.n_mp)
        return remote(
            self.partial.at[peer], self.landed.at[k], self.sems.at[0, k], self.sems.at[1, k], mp=peer
        )

    def spread_copy(self, k, sign):
        at = self.at
        peer = lax.rem(at.mp + at.n_mp + sign * k, at.n_mp)
        place = self.total.at[at.mp if sign == 1 else peer]
        return remote(place, place, self.sems.at[2, k], self.sems.at[3, k], mp=peer)

    def scatter(self):
        for k in range(1, self.at.n_mp):
            self.scatter_copy(k).start()

    def summed(self):
        mine = self.partial[self.at.mp]
        for k in range(1, self.at.n_mp):
            self.scatter_copy(k).wait_recv()
            mine = mine + self.landed[k]
        return mine

    def spread(self, mine):
        self.total[self.at.mp] = mine
        for k in range(1, self.at.n_mp):
            self.spread_copy(k, 1).start()

    def arrive(self):
        for k in range(1, self.at.n_mp):
            self.spread_copy(k, -1).wait_recv()

    def wait_send(self):
        for k in range(1, self.at.n_mp):
            self.scatter_copy(k).wait_send()
            self.spread_copy(k, 1).wait_send()


def side_by_side(a):
    half = a.shape[-2] // 2
    return jnp.concatenate([a[..., :half, :], a[..., half:, :]], axis=-1)


def one_below_other(a):
    half = a.shape[-1] // 2
    return jnp.concatenate([a[..., :half], a[..., half:]], axis=-2)


def pack(a, wide):
    return jnp.concatenate([a[..., :wide], side_by_side(a[..., wide:])], axis=-2)


def unpack(a):
    rows = a.shape[-2] * 2 // 3
    return jnp.concatenate([a[..., :rows, :], one_below_other(a[..., rows:, :])], axis=-1)


def by_devices(a, columns, wide):
    return pack(a.reshape(a.shape[0] // columns, columns, a.shape[1]), wide)


def from_devices(a):
    a = unpack(a)
    return a.reshape(a.shape[0] * a.shape[1], a.shape[2])


def whole_kernel(
    n_dp,
    n_mp,
    rows_hbm,
    queries_hbm,
    keys_hbm,
    values_hbm,
    upstream_hbm,
    down_hbm,
    upq_hbm,
    upkv_hbm,
    slot_ref,
    doc_ref,
    table_ref,
    got_one,
    got_two,
    got_up_a,
    got_up_b,
    flags,
    rows_ref,
    queries_ref,
    keys_ref,
    values_ref,
    upstream_ref,
    down_ref,
    upq_ref,
    upkv_ref,
    send_panels,
    recv_panels,
    send_rows,
    recv_rows,
    send_part,
    recv_part,
    send_two,
    recv_two,
    send_up_a,
    send_up_b,
    recv_up_a,
    recv_up_b,
    partial,
    landed,
    total,
    partial_back,
    landed_back,
    total_back,
    low_one_back,
    recv_low,
    served_rows_turned,
    rows_turned,
    bias,
    grad_query_turned,
    grad_key,
    grad_value,
    send_up_a_back,
    send_up_b_back,
    send_two_back,
    send_one_back,
    load_sems,
    peer_sems,
    plane_sems,
    plane_sems_back,
    to_sems,
    to_sems_recv,
    from_sems,
    from_sems_recv,
    sum_sems,
):
    at = Place(n_dp, n_mp)
    dp = at.dp
    row_total, width = rows_ref.shape
    rank = down_ref.shape[2] // 3
    wide = 2 * rank
    columns = down_ref.shape[1]
    heads = queries_ref.shape[1] // LANES
    per_group = heads // 2
    group_lanes = per_group * LANES
    blocks = slot_ref.shape[0]
    block_rows = row_total // blocks
    plane_columns = width // at.planes
    inverse = 1.0 / float(LANES) ** 0.5

    loads = [
        pltpu.make_async_copy(source, target, load_sems.at[i])
        for i, (source, target) in enumerate(
            [
                (down_hbm, down_ref),
                (upq_hbm, upq_ref),
                (upkv_hbm, upkv_ref),
                (rows_hbm, rows_ref),
                (keys_hbm, keys_ref),
                (values_hbm, values_ref),
                (queries_hbm, queries_ref),
                (upstream_hbm, upstream_ref),
            ]
        )
    ]
    for load in loads:
        load.start()
    arrived = barrier(at)

    late = slot_ref[1].astype(F32)
    early = 1.0 - late
    flags[pl.ds(dp, 1)] = jnp.full((1, 1, LANES), late)
    for load in loads[:4]:
        load.wait()
    rows = rows_ref[...]
    outer_first = rows[:block_rows].astype(F32)
    outer_last = rows[row_total - block_rows :].astype(F32)
    rows_one = outer_first * late + outer_last * early
    for z in range(0, at.planes, 2):
        tile = rows_one[:, z * plane_columns : (z + 2) * plane_columns]
        send_rows[z] = side_by_side(tile[:, :plane_columns])
        send_rows[z + 1] = side_by_side(tile[:, plane_columns:])

    @pl.loop(0, n_dp)
    def _(d):
        first, second = table_ref[0, d], table_ref[1, d]
        a, b = down_ref[first], down_ref[second]
        send_panels[d] = jnp.concatenate(
            [a[:, :wide], b[:, :wide], jnp.concatenate([a[:, wide:], b[:, wide:]], axis=1)],
            axis=0,
        )
        a, b = upq_ref[first], upq_ref[second]
        send_up_a[d, 0] = a[:per_group]
        send_up_a[d, 1] = b[:per_group]
        send_up_a[d, 2] = jnp.concatenate([upkv_ref[first], upkv_ref[second]], axis=0)
        send_up_b[d, 0] = a[per_group:]
        send_up_b[d, 1] = b[per_group:]

    arrived()

    def exchange(index, source, target):
        return Exchange(
            source, target, peer_sems.at[2 * index], peer_sems.at[2 * index + 1], dp, n_dp
        )

    announce = Announce(at, flags, peer_sems.at[0], peer_sems.at[1])
    two_in = exchange(1, send_two, recv_two)
    up_a_in = exchange(2, send_up_a, recv_up_a)
    up_b_in = exchange(3, send_up_b, recv_up_b)
    two_back = exchange(4, send_two_back, got_two)
    up_a_back = exchange(5, send_up_a_back, got_up_a)
    up_b_back = exchange(6, send_up_b_back, got_up_b)
    rows_out = ToWorkers(at, send_rows, recv_rows, to_sems.at[0], to_sems_recv.at[0], False)
    low_out = ToWorkers(at, low_one_back, recv_low, to_sems.at[1], to_sems_recv.at[1], True)
    part_back = FromWorkers(at, send_part, recv_part, from_sems, from_sems_recv)
    panels_in = InPlane(
        at,
        lambda w, m, q: send_panels.at[at.served(w, m, q)],
        lambda w, m, q: recv_panels.at[w, m, q],
        plane_sems.at[0],
        plane_sems.at[1],
    )
    one_back = InPlane(
        at,
        lambda w, m, q: send_one_back.at[w, m, q],
        lambda w, m, q: got_one.at[at.served(w, m, q)],
        plane_sems_back.at[0],
        plane_sems_back.at[1],
    )
    announce.start()
    rows_out.start()
    panels_in.start()
    panels_in.keep()

    rows_two = jnp.concatenate(
        [
            (outer_last * late + outer_first * early).astype(BF16),
            rows[block_rows : row_total - block_rows],
        ],
        axis=0,
    )
    announce.wait_recv()

    @pl.loop(0, n_dp)
    def _(d):
        second = flags[d]
        first = 1.0 - second
        panel = send_panels[d]
        narrow = panel[2 * columns :]
        narrow = narrow[:, :rank] * first[:, :rank] + narrow[:, rank:] * second[:, :rank]
        send_two[d] = jnp.concatenate(
            [
                panel[:columns] * first + panel[columns : 2 * columns] * second,
                side_by_side(narrow),
            ],
            axis=0,
        )

    start_all([[two_in]], n_dp)
    two_in.keep()
    rows_turned[...] = rows_two.T

    lane = lax.broadcasted_iota(jnp.int32, (1, row_total), 1)
    doc_lane = jnp.zeros((1, row_total), jnp.int32)
    for start in range(0, row_total, DOC_ROWS):
        doc_lane = jnp.where(lane >= start, doc_ref[start], doc_lane)
    sub = lax.broadcasted_iota(jnp.int32, (DOC_ROWS, row_total), 0)
    for start in range(0, row_total, DOC_ROWS):
        joined = (doc_lane == doc_ref[start]) & (sub + start <= lane)
        bias[start : start + DOC_ROWS] = jnp.where(joined, 0.0, MASKED).astype(F32)
    in_second = jnp.concatenate(
        [jnp.full((block_rows, LANES), slot_ref[b].astype(F32)) for b in range(blocks)], axis=0
    )
    in_first = 1.0 - in_second

    rows_out.wait_recv()
    panels_in.wait_recv()
    for w in range(at.per):
        served = jnp.concatenate(
            [one_below_other(recv_rows[w, m]) for m in range(n_mp)], axis=1
        ).astype(BF16)
        served_rows_turned[w] = served.T
        panels = jnp.concatenate(
            [
                recv_panels[w, :, :, i * columns : (i + 1) * columns, :].reshape(
                    n_mp * PLANE * columns, LANES
                )
                for i in range(3)
            ],
            axis=1,
        )
        low = dot(served, jnp.concatenate(parts(panels), axis=1), 1, 0)
        low = low[:, : 3 * LANES] + low[:, 3 * LANES :]
        first = flags[at.served(w)]
        second = 1.0 - first
        both = low[:, 2 * LANES :]
        low = jnp.concatenate(
            [
                low[:, :LANES] * first + low[:, LANES : 2 * LANES] * second,
                both[:, :rank] * first[:, :rank] + both[:, rank:] * second[:, :rank],
            ],
            axis=1,
        )
        low = pack(low, wide)
        send_part[w] = low.reshape(n_mp, low.shape[0] // n_mp, LANES)
    part_back.start()
    start_all([[up_a_in], [up_b_in]], n_dp)
    up_a_in.keep()
    up_b_in.keep()
    for load in loads[4:]:
        load.wait()

    two_in.wait_recv()
    low = dot(rows_two, jnp.concatenate(parts(from_devices(recv_two[...])), axis=1), 1, 0)
    low = pack(low[:, : 3 * rank] + low[:, 3 * rank :], wide)
    partial[...] = low.reshape(partial.shape)
    low_sum = SumOverMp(at, partial, landed, total, sum_sems.at[0])
    low_sum.scatter()
    part_back.wait_recv()
    mine_one = recv_part[0]
    for z in range(1, at.planes):
        mine_one = mine_one + recv_part[z]
    two_rows = partial.shape[1]
    one_rows = mine_one.shape[0]
    low_sum.spread(jnp.concatenate([low_sum.summed(), mine_one], axis=0))
    low_sum.arrive()
    low_two = unpack(total[:, :two_rows].reshape(n_mp * two_rows, LANES))
    low_one = unpack(total[:, two_rows:].reshape(n_mp * one_rows, LANES))
    low = jnp.concatenate(
        [
            low_one * late + low_two[:block_rows] * early,
            low_two[block_rows:],
            low_two[:block_rows] * late + low_one * early,
        ],
        axis=0,
    )

    def by_slot(low):
        return jnp.concatenate(
            [low * in_first[:, :rank], low * in_second[:, :rank]], axis=1
        )

    low_q = by_slot(low[:, :rank])
    low_k = by_slot(low[:, rank:wide])
    low_v = by_slot(low[:, wide:])

    def adapted(frozen, low, panel):
        return (frozen.astype(F32) + ADAPTER_SCALE * dot_both(low, panel, 1, 0)).astype(BF16)

    up_a_in.wait_recv()
    up_k = jnp.concatenate([recv_up_a[:, 2, 0, :], recv_up_a[:, 2, 2, :]], axis=0)
    up_v = jnp.concatenate([recv_up_a[:, 2, 1, :], recv_up_a[:, 2, 3, :]], axis=0)
    key = adapted(keys_ref[...], low_k, up_k)
    value = adapted(values_ref[...], low_v, up_v)
    key_turned = key.T
    grad_key[...] = jnp.zeros_like(grad_key)
    grad_value[...] = jnp.zeros_like(grad_value)
    grad_low_q = jnp.zeros((wide, row_total), F32)
    for g, recv_up, send_back in ((0, recv_up_a, send_up_a_back), (1, recv_up_b, send_up_b_back)):
        lanes = slice(g * group_lanes, (g + 1) * group_lanes)
        if g == 1:
            up_b_in.wait_recv()
        panel = jnp.concatenate(
            [
                jnp.concatenate([recv_up[:, 0, h, :], recv_up[:, 1, h, :]], axis=0)
                for h in range(per_group)
            ],
            axis=1,
        )
        query = adapted(queries_ref[:, lanes], low_q, panel)
        upstream = upstream_ref[:, lanes]

        def stacked(a, first):
            return jnp.concatenate(
                [
                    a[first : first + block_rows, h * LANES : (h + 1) * LANES]
                    for h in range(per_group)
                ],
                axis=0,
            )

        for b in range(blocks):
            first, last = b * block_rows, (b + 1) * block_rows
            query_b, upstream_b = stacked(query, first), stacked(upstream, first)
            mask = jnp.concatenate([bias[0:last, first:last]] * per_group, axis=1)
            scores = dot(key[:last], query_b, 1, 1) * inverse + mask
            weights = jnp.exp(scores - jnp.max(scores, axis=0, keepdims=True))
            probs = weights * (1.0 / jnp.sum(weights, axis=0, keepdims=True))
            grad_probs = dot(value[:last], upstream_b, 1, 1)
            inner = jnp.sum(probs * grad_probs, axis=0, keepdims=True)
            grad_scores = (probs * (grad_probs - inner) * inverse).astype(BF16)
            grad_key[0:last] += dot(grad_scores, query_b, 1, 0)
            grad_value[0:last] += dot(probs.astype(BF16), upstream_b, 1, 0)
            turned = dot(key_turned[:, :last], grad_scores, 1, 0)
            for h in range(per_group):
                grad_query_turned[h * LANES : (h + 1) * LANES, first:last] = turned[
                    :, h * block_rows : (h + 1) * block_rows
                ]
        grad_query = grad_query_turned[...]
        term = ADAPTER_SCALE * dot_both(grad_query, low_q, 1, 0)
        for h in range(per_group):
            turned = term[h * LANES : (h + 1) * LANES].T
            send_back[:, 0, h, :] = turned[:rank]
            send_back[:, 1, h, :] = turned[rank:]
        grad_low_q = grad_low_q + dot_both(panel, grad_query, 1, 0)
        if g == 0:
            start_all([[up_a_back]], n_dp)

    def of_slot(grad):
        return ADAPTER_SCALE * (
            grad[:, :rank] * in_first[:, :rank] + grad[:, rank:] * in_second[:, :rank]
        )

    grad_k, grad_v = grad_key[...], grad_value[...]
    grad_low = jnp.concatenate(
        [
            of_slot(grad_low_q.T),
            of_slot(dot_both(grad_k, up_k, 1, 1)),
            of_slot(dot_both(grad_v, up_v, 1, 1)),
        ],
        axis=1,
    )
    outer_first = grad_low[:block_rows]
    outer_last = grad_low[row_total - block_rows :]
    grad_one = pack(outer_first * late + outer_last * early, wide)
    grad_two = pack(
        jnp.concatenate(
            [
                outer_last * late + outer_first * early,
                grad_low[block_rows : row_total - block_rows],
            ],
            axis=0,
        ),
        wide,
    )
    partial_back[...] = jnp.concatenate(
        [grad_two.reshape(n_mp, two_rows, LANES), grad_one.reshape(n_mp, one_rows, LANES)],
        axis=1,
    )
    grad_sum = SumOverMp(at, partial_back, landed_back, total_back, sum_sems.at[1])
    term = ADAPTER_SCALE * dot_both(low_k, grad_k, 0, 0)
    send_up_b_back[:, 2, 0, :] = term[:rank]
    send_up_b_back[:, 2, 2, :] = term[rank:]
    term = ADAPTER_SCALE * dot_both(low_v, grad_v, 0, 0)
    send_up_b_back[:, 2, 1, :] = term[:rank]
    send_up_b_back[:, 2, 3, :] = term[rank:]
    grad_sum.scatter()
    start_all([[up_b_back]], n_dp)
    mine = grad_sum.summed()
    low_one_back[...] = mine[two_rows:]
    grad_sum.spread(mine[:two_rows])
    low_out.start()
    up_a_back.keep()
    up_b_back.keep()
    grad_sum.arrive()
    grads = unpack(total_back[...].reshape(n_mp * two_rows, LANES))
    term = dot(rows_turned[...], jnp.concatenate(parts(grads), axis=1), 1, 0)
    send_two_back[...] = by_devices(term[:, : 3 * rank] + term[:, 3 * rank :], columns, wide)
    start_all([[two_back]], n_dp)
    two_back.keep()

    low_out.wait_recv()
    for w in range(at.per):
        grads = unpack(recv_low[w].reshape(n_mp * one_rows, LANES))
        term = dot(served_rows_turned[w], jnp.concatenate(parts(grads), axis=1), 1, 0)
        term = by_devices(term[:, : 3 * rank] + term[:, 3 * rank :], columns, wide)
        send_one_back[w] = term.reshape(n_mp, PLANE, term.shape[1], LANES)
    one_back.start()
    one_back.keep()

    for one in (
        announce,
        rows_out,
        panels_in,
        two_in,
        part_back,
        up_a_in,
        up_b_in,
        low_sum,
        grad_sum,
        low_out,
    ):
        one.wait_send()
    for one in (up_a_back, up_b_back, one_back, two_back):
        one.wait_recv()
        one.wait_send()


def owner_kernel(
    one_ref, two_ref, up_a_ref, up_b_ref, flags_ref, table_ref, out_down, out_upq, out_upkv
):
    tenants, columns = out_down.shape[0], out_down.shape[1]
    rank = out_down.shape[2] // 3
    n_dp = one_ref.shape[0]
    per_group = up_a_ref.shape[2]
    tenant = lax.broadcasted_iota(jnp.int32, (tenants, n_dp), 0)
    owned = [
        jnp.where(tenant == table_ref[slot : slot + 1, :], 1.0, 0.0).astype(F32)
        for slot in range(2)
    ]
    late = flags_ref[:, 0, :].T[0:1, :]
    early = 1.0 - late
    owned_down = jnp.concatenate(
        [owned[0] * late + owned[1] * early, owned[1] * late + owned[0] * early], axis=1
    ).astype(BF16)
    owned_up = jnp.concatenate(owned, axis=1).astype(BF16)

    def spread(hot, count, pair, store):
        for start in range(0, count, 4):
            span = range(start, min(start + 4, count))
            terms = jnp.concatenate(
                [jnp.concatenate(pair(r), axis=0) for r in span], axis=1
            )
            total = dot_exact_left(hot, terms, 1, 0)
            for n, r in enumerate(span):
                store(r, total[:, n * LANES : (n + 1) * LANES])

    def store_down(r, total):
        if r < columns:
            out_down[:, r, 0:LANES] = total
        else:
            out_down[:, r - columns, LANES : LANES + rank] = total[:, :rank]
            out_down[:, r - columns // 2, LANES : LANES + rank] = total[:, rank:]

    spread(
        owned_down, one_ref.shape[1], lambda r: [one_ref[:, r, :], two_ref[:, r, :]], store_down
    )
    for g, ref in ((0, up_a_ref), (1, up_b_ref)):

        def store_upq(r, total, g=g):
            out_upq[:, g * per_group + r, :] = total

        spread(owned_up, per_group, lambda r, ref=ref: [ref[:, 0, r, :], ref[:, 1, r, :]], store_upq)

    def store_upkv(r, total):
        out_upkv[:, r, :] = total

    spread(owned_up, 2, lambda r: [up_b_ref[:, 2, r, :], up_b_ref[:, 2, 2 + r, :]], store_upkv)


def on_device(
    normed_input_rows,
    frozen_queries,
    frozen_keys,
    frozen_values,
    attention_output_gradient,
    adapter_down_weight,
    adapter_up_query,
    adapter_up_key_value,
    document_numbers,
    block_tenant_slot,
    shard_tenant_table,
    *,
    n_dp,
    n_mp,
):
    row_total = normed_input_rows.shape[0]
    tenants, columns, three_rank = adapter_down_weight.shape
    heads = frozen_queries.shape[1] // LANES
    upq = adapter_up_query.reshape(tenants, heads, LANES)
    upkv = adapter_up_key_value.reshape(tenants, 2, LANES)
    table = shard_tenant_table.T
    vmem = pl.BlockSpec(memory_space=pltpu.VMEM)
    smem = pl.BlockSpec(memory_space=pltpu.SMEM)
    loaded = (
        normed_input_rows,
        frozen_queries,
        frozen_keys,
        frozen_values,
        attention_output_gradient,
        adapter_down_weight,
        upq,
        upkv,
    )
    width = normed_input_rows.shape[1]
    block_rows = row_total // block_tenant_slot.shape[0]
    planes = n_dp // PLANE
    per = planes // n_mp
    one_rows = block_rows * three_rank // LANES // n_mp
    two_rows = 2 * one_rows
    all_rows = one_rows + two_rows
    piece = columns * three_rank // LANES
    send_rows_shape = (planes, block_rows * (width // planes) // LANES, LANES)

    def f32(*shape):
        return pltpu.VMEM(shape, F32)

    def dma(*shape):
        return pltpu.SemaphoreType.DMA(shape)

    outs = [
        (n_dp, piece, LANES),
        (n_dp, piece, LANES),
        (n_dp, 2, heads // 2, LANES),
        (n_dp, 3, heads // 2, LANES),
        (n_dp, 1, LANES),
    ]
    got = pl.pallas_call(
        functools.partial(whole_kernel, n_dp, n_mp),
        out_shape=[jax.ShapeDtypeStruct(s, F32) for s in outs],
        in_specs=[pl.BlockSpec(memory_space=pl.ANY)] * 8 + [smem] * 3,
        out_specs=[vmem] * len(outs),
        scratch_shapes=[
            *(pltpu.VMEM(a.shape, a.dtype) for a in loaded),
            f32(n_dp, 3 * columns, LANES),
            f32(per, n_mp, PLANE, 3 * columns, LANES),
            f32(*send_rows_shape),
            f32(per, n_mp, *send_rows_shape[1:]),
            f32(per, n_mp, one_rows, LANES),
            f32(planes, one_rows, LANES),
            f32(n_dp, piece, LANES),
            f32(n_dp, piece, LANES),
            f32(n_dp, 3, heads // 2, LANES),
            f32(n_dp, 2, heads // 2, LANES),
            f32(n_dp, 3, heads // 2, LANES),
            f32(n_dp, 2, heads // 2, LANES),
            f32(n_mp, two_rows, LANES),
            f32(n_mp, two_rows, LANES),
            f32(n_mp, all_rows, LANES),
            f32(n_mp, all_rows, LANES),
            f32(n_mp, all_rows, LANES),
            f32(n_mp, two_rows, LANES),
            f32(one_rows, LANES),
            f32(per, n_mp, one_rows, LANES),
            pltpu.VMEM((per, n_mp * PLANE * columns, block_rows), BF16),
            pltpu.VMEM((width, row_total - block_rows), BF16),
            f32(row_total, row_total),
            f32(heads // 2 * LANES, row_total),
            f32(row_total, LANES),
            f32(row_total, LANES),
            f32(n_dp, 2, heads // 2, LANES),
            f32(n_dp, 3, heads // 2, LANES),
            f32(n_dp, piece, LANES),
            f32(per, n_mp, PLANE, piece, LANES),
            dma(len(loaded)),
            dma(14, n_dp),
            dma(2, PLANE * n_mp, per),
            dma(2, PLANE * n_mp, per),
            dma(2, planes),
            dma(2, per, n_mp),
            dma(per, n_mp),
            dma(planes),
            dma(2, 4, n_mp),
        ],
        compiler_params=pltpu.CompilerParams(
            collective_id=0, has_side_effects=True, vmem_limit_bytes=60 * 1024 * 1024
        ),
        name="whole",
    )(*loaded, block_tenant_slot, document_numbers, table)
    grad_down, grad_upq, grad_upkv = pl.pallas_call(
        owner_kernel,
        out_shape=[
            jax.ShapeDtypeStruct(adapter_down_weight.shape, F32),
            jax.ShapeDtypeStruct(upq.shape, F32),
            jax.ShapeDtypeStruct(upkv.shape, F32),
        ],
        in_specs=[vmem] * 6,
        out_specs=[vmem] * 3,
        name="owner",
    )(*got, table)
    return (
        grad_down,
        grad_upq.reshape(adapter_up_query.shape),
        grad_upkv.reshape(adapter_up_key_value.shape),
    )


def solution(mesh):
    placed = (
        P("dp", "mp"),
        P("dp", "mp"),
        P("dp", "mp"),
        P("dp", "mp"),
        P("dp", "mp"),
        P(None, ("mp", "dp"), None),
        P(None, "dp", "mp"),
        P(None, "dp", "mp", None),
        P("dp"),
        P("dp"),
        P(),
    )
    return jax.shard_map(
        functools.partial(on_device, n_dp=mesh.shape["dp"], n_mp=mesh.shape["mp"]),
        mesh=mesh,
        in_specs=placed,
        out_specs=(P(None, ("mp", "dp"), None), P(None, "dp", "mp"), P(None, "dp", "mp", None)),
        check_vma=False,
    )
```

time: 232 us -> 214 us (0.922)
  Pallas kernels: 230 us -> 213 us
    pallas_call x1, Pallas kernels: 226 us -> 208 us  [on_device(): pl.pallas_call(functools.partial(whole_kernel, n_dp, n_mp), out_shape=[ja...]
where the time goes in v3:
time: 214 us
  Pallas kernels  213 us (100%)
    pallas_call x1, Pallas kernels, on_device(): pl.pallas_call(functools.partial(whole_kernel, n_dp, n_mp), out_shape=[ja...  208 us
    pallas_call x1, Pallas kernels, on_device(): pl.pallas_call(owner_kernel, out_shape=[jax.ShapeDtypeStruct(adapter_down...  5.11 us

profile of v3, /device:TPU:1, one launch (start us, length us, event | category | flops | bytes accessed | tf_op | source)
XLA Modules:
  0.0 213.5 jit_solution(15478832814585726416)
XLA Ops:
  0.6 207.8 %whole.1 = (f32[64,24,128]{2,1,0:T(8,128)}, f32[64,24,128]{2,1,0:T(8,128)}, f32[64,2,4,128]{3,2,1,0:T(4,128)}, f32[64,3,4,128]{3,2,1,0:T(4,128)}, f32[64,1,128]{2,1,0:T(1,128)}) custom-call(bf16[384,1024]{1,0:T(8,128)(2,1)} %rows_hbm.1, bf16[384,1024]{1,0:T(8,128)(2,1)} %queries_hbm.1, bf16[384,128]{1,0:T(8,128)(2,1)} %keys_hbm.1, ...), custom_call_target="tpu_custom_call" | custom-call | tf_op jit(solution)/shard_map/whole/pallas_call | solution.py:931
  208.4 5.1 %owner.1 = (f32[64,16,192]{2,1,0:T(8,128)}, f32[64,8,128]{2,1,0:T(8,128)}, f32[64,2,128]{2,1,0:T(2,128)}) custom-call(f32[64,24,128]{2,1,0:T(8,128)} %get-tuple-element.11.one_ref, f32[64,24,128]{2,1,0:T(8,128)} %get-tuple-element.12.two_ref, f32[64,2,4,128]{3,2,1,0:T(4,128)} %get-tuple-element.13.up_a_ref, f32[64,3,4,128]{3,2,1,0:T(4,128)} %get-tuple-element.14.up_b_ref, ...), custom_call_target="tpu_custom_call" | custom-call | tf_op jit(solution)/shard_map/owner/pallas_call | solution.py:983

commit v4 on v3

--- a/solution.py
+++ b/solution.py
@@ -37,6 +37,10 @@
     return dot(a_high, b_high, ca, cb) + (dot(a_high, b_low, ca, cb) + dot(a_low, b_high, ca, cb))
 
 
+def wrap(x, n):
+    return jnp.where(x >= n, x - n, x)
+
+
 def signal(sem, **device):
     pl.semaphore_signal(sem, inc=1, device_id=device, device_id_type=MESH)
 
@@ -49,17 +53,18 @@
         self.dp, self.mp = lax.axis_index("dp"), lax.axis_index("mp")
         self.z, self.q = lax.div(self.dp, PLANE), lax.rem(self.dp, PLANE)
         self.worker_slot = lax.div(self.z, n_mp)
+        self.z_mp = lax.rem(self.z, n_mp)
         self.is_own_worker = self.worker_mp(self.z) == self.mp
 
     def worker_mp(self, z):
-        return lax.rem(self.z + z, self.n_mp)
+        return wrap(self.z_mp + wrap(z, self.n_mp), self.n_mp)
 
     def worker(self, dz):
-        z = lax.rem(self.z + dz, self.planes)
+        z = wrap(self.z + dz, self.planes)
         return z, {"dp": z * PLANE + self.q, "mp": self.worker_mp(z)}
 
     def served_z(self, w, m):
-        return lax.rem(m + self.planes - self.z, self.n_mp) + w * self.n_mp
+        return wrap(m + self.n_mp - self.z_mp, self.n_mp) + w * self.n_mp
 
     def served(self, w, m=None, q=None):
         m, q = (self.mp, self.q) if m is None else (m, q)
@@ -68,11 +73,17 @@
     def serves_own_plane(self, w):
         return self.served_z(w, self.mp) == self.z
 
-    def mate(self, k, sign):
-        dq, dm = lax.div(k, self.n_mp), lax.rem(k, self.n_mp)
-        q = lax.rem(self.q + PLANE + sign * dq, PLANE)
-        m = lax.rem(self.mp + self.n_mp + sign * dm, self.n_mp)
-        return q, m
+    def mate(self, dq, dm, sign):
+        if sign == 1:
+            return wrap(self.q + dq, PLANE), wrap(self.mp + dm, self.n_mp)
+        return wrap(self.q + PLANE - dq, PLANE), wrap(self.mp + self.n_mp - dm, self.n_mp)
+
+    def mates(self, act):
+        for dq in range(PLANE):
+
+            @pl.loop(1 if dq == 0 else 0, self.n_mp)
+            def _(dm):
+                act(dq, dm)
 
 
 def barrier(at):
@@ -80,17 +91,16 @@
 
     @pl.loop(1, at.n_dp)
     def _(k):
-        signal(sem, dp=lax.rem(at.dp + k, at.n_dp))
+        signal(sem, dp=wrap(at.dp + k, at.n_dp))
 
     for k in range(1, at.n_mp):
-        signal(sem, mp=lax.rem(at.mp + k, at.n_mp))
-
-    @pl.loop(at.n_mp, PLANE * at.n_mp)
-    def _(k):
-        q, m = at.mate(k, 1)
-
-        @pl.when(m != at.mp)
-        def _():
+        signal(sem, mp=wrap(at.mp + k, at.n_mp))
+
+    for dq in range(1, PLANE):
+
+        @pl.loop(1, at.n_mp)
+        def _(dm):
+            q, m = at.mate(dq, dm, 1)
             signal(sem, dp=at.z * PLANE + q, mp=m)
 
     @pl.loop(1, at.planes)
@@ -228,62 +238,66 @@
 
 
 class InPlane:
-    def __init__(self, at, pick, place, send, recv):
-        self.at, self.pick, self.place, self.send, self.recv = at, pick, place, send, recv
-
-    def copy(self, k, w, sign):
+    def __init__(self, at, source, target, pick, place, send, recv):
+        self.at, self.source, self.target = at, source, target
+        self.pick, self.place, self.send, self.recv = pick, place, send, recv
+
+    def copy(self, dq, dm, w):
         at = self.at
-        q, m = at.mate(k, sign)
-        target = self.place(w, at.mp, at.q) if sign == 1 else self.place(w, m, q)
-        source = self.pick(w, m, q) if sign == 1 else target
+        q, m = at.mate(dq, dm, 1)
         return remote(
-            source, target, self.send.at[k, w], self.recv.at[k, w], dp=at.z * PLANE + q, mp=m
-        )
-
-    def each(self, sign, act):
-        @pl.loop(1, PLANE * self.at.n_mp)
-        def _(k):
+            self.pick(w, m, q),
+            self.place(w, at.mp, at.q),
+            self.send,
+            self.recv,
+            dp=at.z * PLANE + q,
+            mp=m,
+        )
+
+    def start(self):
+        def act(dq, dm):
             for w in range(self.at.per):
-                act(self.copy(k, w, sign))
-
-    def start(self):
-        self.each(1, lambda copy: copy.start())
+                self.copy(dq, dm, w).start()
+
+        self.at.mates(act)
 
     def keep(self):
         at = self.at
         for w in range(at.per):
             self.place(w, at.mp, at.q)[...] = self.pick(w, at.mp, at.q)[...]
 
+    def all(self, ref):
+        ref = ref.at[pl.ds(0, self.at.per * (PLANE * self.at.n_mp - 1))]
+        return remote(ref, ref, self.send, self.recv, dp=wrap(self.at.dp + 1, self.at.n_dp))
+
     def wait_recv(self):
-        self.each(-1, lambda copy: copy.wait_recv())
+        self.all(self.target).wait_recv()
 
     def wait_send(self):
-        self.each(1, lambda copy: copy.wait_send())
+        self.all(self.source).wait_send()
 
 
 class Announce:
     def __init__(self, at, ref, send, recv):
         self.at, self.ref, self.send, self.recv = at, ref, send, recv
 
-    def copy(self, k, sign):
+    def start(self):
         at = self.at
-        peer = lax.rem(at.dp + at.n_dp + sign * k, at.n_dp)
-        place = self.ref.at[at.dp if sign == 1 else peer]
-        return remote(place, place, self.send.at[k], self.recv.at[k], dp=peer)
-
-    def each(self, sign, act):
-        @pl.loop(1, self.at.n_dp)
+        place = self.ref.at[at.dp]
+
+        @pl.loop(1, at.n_dp)
         def _(k):
-            act(self.copy(k, sign))
-
-    def start(self):
-        self.each(1, lambda copy: copy.start())
+            remote(place, place, self.send, self.recv, dp=wrap(at.dp + k, at.n_dp)).start()
+
+    def all(self):
+        ref = self.ref.at[pl.ds(0, self.at.n_dp - 1)]
+        return remote(ref, ref, self.send, self.recv, dp=wrap(self.at.dp + 1, self.at.n_dp))
 
     def wait_recv(self):
-        self.each(-1, lambda copy: copy.wait_recv())
+        self.all().wait_recv()
 
     def wait_send(self):
-        self.each(1, lambda copy: copy.wait_send())
+        self.all().wait_send()
 
 
 class Exchange:
@@ -291,43 +305,43 @@
         self.source, self.target, self.send, self.recv = source, target, send, recv
         self.dp, self.n_dp = dp, n_dp
 
-    def piece(self, k, peer, slot):
-        return pltpu.make_async_remote_copy(
-            src_ref=self.source.at[peer],
-            dst_ref=self.target.at[slot],
-            send_sem=self.send.at[k],
-            recv_sem=self.recv.at[k],
-            device_id={"dp": peer},
-            device_id_type=MESH,
-        )
-
     def start(self, k):
-        self.piece(k, lax.rem(self.dp + k, self.n_dp), self.dp).start()
+        peer = wrap(self.dp + k, self.n_dp)
+        remote(
+            self.source.at[peer], self.target.at[self.dp], self.send, self.recv, dp=peer
+        ).start()
 
     def keep(self):
         self.target[pl.ds(self.dp, 1)] = self.source[pl.ds(self.dp, 1)]
 
+    def all(self):
+        pieces = pl.ds(0, self.n_dp - 1)
+        return remote(
+            self.source.at[pieces],
+            self.target.at[pieces],
+            self.send,
+            self.recv,
+            dp=wrap(self.dp + 1, self.n_dp),
+        )
+
     def wait_recv(self):
-        @pl.loop(1, self.n_dp)
-        def _(k):
-            origin = lax.rem(self.dp + self.n_dp - k, self.n_dp)
-            self.piece(k, origin, origin).wait_recv()
+        self.all().wait_recv()
 
     def wait_send(self):
-        @pl.loop(1, self.n_dp)
-        def _(k):
-            self.piece(k, lax.rem(self.dp + k, self.n_dp), self.dp).wait_send()
+        self.all().wait_send()
 
 
 def start_all(exchanges, n_dp):
     for group in exchanges:
 
-        @pl.loop(0, n_dp - 1)
-        def _(i):
-            half = lax.div(i + 2, 2)
-            k = jnp.where(lax.rem(i, 2) == 0, half, n_dp - half)
+        @pl.loop(1, n_dp // 2)
+        def _(k):
             for exchange in group:
                 exchange.start(k)
+                exchange.start(n_dp - k)
+
+        for exchange in group:
+            exchange.start(n_dp // 2)
 
 
 class SumOverMp:
@@ -335,14 +349,14 @@
         self.at, self.partial, self.landed, self.total, self.sems = at, partial, landed, total, sems
 
     def scatter_copy(self, k):
-        peer = lax.rem(self.at.mp + k, self.at.n_mp)
+        peer = wrap(self.at.mp + k, self.at.n_mp)
         return remote(
             self.partial.at[peer], self.landed.at[k], self.sems.at[0, k], self.sems.at[1, k], mp=peer
         )
 
     def spread_copy(self, k, sign):
         at = self.at
-        peer = lax.rem(at.mp + at.n_mp + sign * k, at.n_mp)
+        peer = wrap(at.mp + (k if sign == 1 else at.n_mp - k), at.n_mp)
         place = self.total.at[at.mp if sign == 1 else peer]
         return remote(place, place, self.sems.at[2, k], self.sems.at[3, k], mp=peer)
 
@@ -460,7 +474,6 @@
     load_sems,
     peer_sems,
     plane_sems,
-    plane_sems_back,
     to_sems,
     to_sems_recv,
     from_sems,
@@ -514,7 +527,7 @@
         send_rows[z] = side_by_side(tile[:, :plane_columns])
         send_rows[z + 1] = side_by_side(tile[:, plane_columns:])
 
-    @pl.loop(0, n_dp)
+    @pl.loop(0, n_dp, unroll=4)
     def _(d):
         first, second = table_ref[0, d], table_ref[1, d]
         a, b = down_ref[first], down_ref[second]
@@ -548,17 +561,21 @@
     part_back = FromWorkers(at, send_part, recv_part, from_sems, from_sems_recv)
     panels_in = InPlane(
         at,
+        send_panels,
+        recv_panels,
         lambda w, m, q: send_panels.at[at.served(w, m, q)],
-        lambda w, m, q: recv_panels.at[w, m, q],
+        lambda w, m, q: recv_panels.at[(w * n_mp + m) * PLANE + q],
         plane_sems.at[0],
         plane_sems.at[1],
     )
     one_back = InPlane(
         at,
-        lambda w, m, q: send_one_back.at[w, m, q],
+        send_one_back,
+        got_one,
+        lambda w, m, q: send_one_back.at[(w * n_mp + m) * PLANE + q],
         lambda w, m, q: got_one.at[at.served(w, m, q)],
-        plane_sems_back.at[0],
-        plane_sems_back.at[1],
+        plane_sems.at[2],
+        plane_sems.at[3],
     )
     announce.start()
     rows_out.start()
@@ -574,7 +591,7 @@
     )
     announce.wait_recv()
 
-    @pl.loop(0, n_dp)
+    @pl.loop(0, n_dp, unroll=4)
     def _(d):
         second = flags[d]
         first = 1.0 - second
@@ -615,9 +632,9 @@
         served_rows_turned[w] = served.T
         panels = jnp.concatenate(
             [
-                recv_panels[w, :, :, i * columns : (i + 1) * columns, :].reshape(
-                    n_mp * PLANE * columns, LANES
-                )
+                recv_panels[
+                    w * n_mp * PLANE : (w + 1) * n_mp * PLANE, i * columns : (i + 1) * columns, :
+                ].reshape(n_mp * PLANE * columns, LANES)
                 for i in range(3)
             ],
             axis=1,
@@ -796,8 +813,9 @@
     for w in range(at.per):
         grads = unpack(recv_low[w].reshape(n_mp * one_rows, LANES))
         term = dot(served_rows_turned[w], jnp.concatenate(parts(grads), axis=1), 1, 0)
-        term = by_devices(term[:, : 3 * rank] + term[:, 3 * rank :], columns, wide)
-        send_one_back[w] = term.reshape(n_mp, PLANE, term.shape[1], LANES)
+        send_one_back[w * n_mp * PLANE : (w + 1) * n_mp * PLANE] = by_devices(
+            term[:, : 3 * rank] + term[:, 3 * rank :], columns, wide
+        )
     one_back.start()
     one_back.keep()
 
@@ -936,7 +954,7 @@
         scratch_shapes=[
             *(pltpu.VMEM(a.shape, a.dtype) for a in loaded),
             f32(n_dp, 3 * columns, LANES),
-            f32(per, n_mp, PLANE, 3 * columns, LANES),
+            f32(per * n_mp * PLANE, 3 * columns, LANES),
             f32(*send_rows_shape),
             f32(per, n_mp, *send_rows_shape[1:]),
             f32(per, n_mp, one_rows, LANES),
@@ -964,11 +982,10 @@
             f32(n_dp, 2, heads // 2, LANES),
             f32(n_dp, 3, heads // 2, LANES),
             f32(n_dp, piece, LANES),
-            f32(per, n_mp, PLANE, piece, LANES),
+            f32(per * n_mp * PLANE, piece, LANES),
             dma(len(loaded)),
-            dma(14, n_dp),
-            dma(2, PLANE * n_mp, per),
-            dma(2, PLANE * n_mp, per),
+            dma(14),
+            dma(4),
             dma(2, planes),
             dma(2, per, n_mp),
             dma(per, n_mp),

time: 214 us -> 203 us (0.949)
  Pallas kernels: 213 us -> 203 us
    pallas_call x1, Pallas kernels: 208 us -> 198 us  [on_device(): pl.pallas_call(functools.partial(whole_kernel, n_dp, n_mp), out_shape=[ja...]
where the time goes in v4:
time: 203 us
  Pallas kernels  203 us (100%)
    pallas_call x1, Pallas kernels, on_device(): pl.pallas_call(functools.partial(whole_kernel, n_dp, n_mp), out_shape=[ja...  198 us
    pallas_call x1, Pallas kernels, on_device(): pl.pallas_call(owner_kernel, out_shape=[jax.ShapeDtypeStruct(adapter_down...  5.11 us

profile of v4, /device:TPU:1, one launch (start us, length us, event | category | flops | bytes accessed | tf_op | source)
XLA Modules:
  0.0 203.3 jit_solution(16805810654723757148)
XLA Ops:
  0.6 197.5 %whole.1 = (f32[64,24,128]{2,1,0:T(8,128)}, f32[64,24,128]{2,1,0:T(8,128)}, f32[64,2,4,128]{3,2,1,0:T(4,128)}, f32[64,3,4,128]{3,2,1,0:T(4,128)}, f32[64,1,128]{2,1,0:T(1,128)}) custom-call(bf16[384,1024]{1,0:T(8,128)(2,1)} %rows_hbm.1, bf16[384,1024]{1,0:T(8,128)(2,1)} %queries_hbm.1, bf16[384,128]{1,0:T(8,128)(2,1)} %keys_hbm.1, ...), custom_call_target="tpu_custom_call" | custom-call | tf_op jit(solution)/shard_map/whole/pallas_call | solution.py:949
  198.2 5.1 %owner.1 = (f32[64,16,192]{2,1,0:T(8,128)}, f32[64,8,128]{2,1,0:T(8,128)}, f32[64,2,128]{2,1,0:T(2,128)}) custom-call(f32[64,24,128]{2,1,0:T(8,128)} %get-tuple-element.11.one_ref, f32[64,24,128]{2,1,0:T(8,128)} %get-tuple-element.12.two_ref, f32[64,2,4,128]{3,2,1,0:T(4,128)} %get-tuple-element.13.up_a_ref, f32[64,3,4,128]{3,2,1,0:T(4,128)} %get-tuple-element.14.up_b_ref, ...), custom_call_target="tpu_custom_call" | custom-call | tf_op jit(solution)/shard_map/owner/pallas_call | solution.py:1000

commit v5 on v4

--- a/solution.py
+++ b/solution.py
@@ -838,8 +838,36 @@
 
 
 def owner_kernel(
-    one_ref, two_ref, up_a_ref, up_b_ref, flags_ref, table_ref, out_down, out_upq, out_upkv
+    one_hbm,
+    two_hbm,
+    up_a_hbm,
+    up_b_hbm,
+    flags_ref,
+    table_ref,
+    down_hbm,
+    upq_hbm,
+    upkv_hbm,
+    one_ref,
+    two_ref,
+    up_a_ref,
+    up_b_ref,
+    out_down,
+    out_upq,
+    out_upkv,
+    sems,
 ):
+    pairs = [
+        (up_a_hbm, up_a_ref),
+        (up_b_hbm, up_b_ref),
+        (one_hbm, one_ref),
+        (two_hbm, two_ref),
+        (out_upq, upq_hbm),
+        (out_upkv, upkv_hbm),
+        (out_down, down_hbm),
+    ]
+    copies = [pltpu.make_async_copy(a, b, sems.at[i]) for i, (a, b) in enumerate(pairs)]
+    for copy in copies[:4]:
+        copy.start()
     tenants, columns = out_down.shape[0], out_down.shape[1]
     rank = out_down.shape[2] // 3
     n_dp = one_ref.shape[0]
@@ -873,20 +901,29 @@
             out_down[:, r - columns, LANES : LANES + rank] = total[:, :rank]
             out_down[:, r - columns // 2, LANES : LANES + rank] = total[:, rank:]
 
+    for copy in copies[:2]:
+        copy.wait()
+    for g, ref in ((0, up_a_ref), (1, up_b_ref)):
+
+        def store_upq(r, total, g=g):
+            out_upq[:, g * per_group + r, :] = total
+
+        spread(owned_up, per_group, lambda r, ref=ref: [ref[:, 0, r, :], ref[:, 1, r, :]], store_upq)
+
+    def store_upkv(r, total):
+        out_upkv[:, r, :] = total
+
+    spread(owned_up, 2, lambda r: [up_b_ref[:, 2, r, :], up_b_ref[:, 2, 2 + r, :]], store_upkv)
+    for copy in copies[4:6]:
+        copy.start()
+    for copy in copies[2:4]:
+        copy.wait()
     spread(
         owned_down, one_ref.shape[1], lambda r: [one_ref[:, r, :], two_ref[:, r, :]], store_down
     )
-    for g, ref in ((0, up_a_ref), (1, up_b_ref)):
-
-        def store_upq(r, total, g=g):
-            out_upq[:, g * per_group + r, :] = total
-
-        spread(owned_up, per_group, lambda r, ref=ref: [ref[:, 0, r, :], ref[:, 1, r, :]], store_upq)
-
-    def store_upkv(r, total):
-        out_upkv[:, r, :] = total
-
-    spread(owned_up, 2, lambda r: [up_b_ref[:, 2, r, :], up_b_ref[:, 2, 2 + r, :]], store_upkv)
+    copies[6].start()
+    for copy in copies[4:]:
+        copy.wait()
 
 
 def on_device(
@@ -1004,8 +1041,15 @@
             jax.ShapeDtypeStruct(upq.shape, F32),
             jax.ShapeDtypeStruct(upkv.shape, F32),
         ],
-        in_specs=[vmem] * 6,
-        out_specs=[vmem] * 3,
+        in_specs=[pl.BlockSpec(memory_space=pl.ANY)] * 4 + [vmem] * 2,
+        out_specs=[pl.BlockSpec(memory_space=pl.ANY)] * 3,
+        scratch_shapes=[
+            *(f32(*shape) for shape in outs[:4]),
+            f32(*adapter_down_weight.shape),
+            f32(*upq.shape),
+            f32(*upkv.shape),
+            dma(7),
+        ],
         name="owner",
     )(*got, table)
     return (

time: 203 us -> 204 us (level)
  no operation moved by 1% of the time
where the time goes in v5:
time: 204 us
  Pallas kernels  203 us (100%)
    pallas_call x1, Pallas kernels, on_device(): pl.pallas_call(functools.partial(whole_kernel, n_dp, n_mp), out_shape=[ja...  198 us
    pallas_call x1, Pallas kernels, on_device(): pl.pallas_call(owner_kernel, out_shape=[jax.ShapeDtypeStruct(adapter_down...  5.48 us

profile of v5, /device:TPU:1, one launch (start us, length us, event | category | flops | bytes accessed | tf_op | source)
XLA Modules:
  0.0 203.8 jit_solution(6443599599513344059)
XLA Ops:
  0.6 197.5 %whole.1 = (f32[64,24,128]{2,1,0:T(8,128)}, f32[64,24,128]{2,1,0:T(8,128)}, f32[64,2,4,128]{3,2,1,0:T(4,128)}, f32[64,3,4,128]{3,2,1,0:T(4,128)}, f32[64,1,128]{2,1,0:T(1,128)}) custom-call(bf16[384,1024]{1,0:T(8,128)(2,1)} %rows_hbm.1, bf16[384,1024]{1,0:T(8,128)(2,1)} %queries_hbm.1, bf16[384,128]{1,0:T(8,128)(2,1)} %keys_hbm.1, ...), custom_call_target="tpu_custom_call" | custom-call | tf_op jit(solution)/shard_map/whole/pallas_call | solution.py:986
  198.2 5.5 %owner.1 = (f32[64,16,192]{2,1,0:T(8,128)}, f32[64,8,128]{2,1,0:T(8,128)}, f32[64,2,128]{2,1,0:T(2,128)}) custom-call(f32[64,24,128]{2,1,0:T(8,128)} %get-tuple-element.11.one_hbm, f32[64,24,128]{2,1,0:T(8,128)} %get-tuple-element.12.two_hbm, f32[64,2,4,128]{3,2,1,0:T(4,128)} %get-tuple-element.13.up_a_hbm, f32[64,3,4,128]{3,2,1,0:T(4,128)} %get-tuple-element.14.up_b_hbm, ...), custom_call_target="tpu_custom_call" | custom-call | tf_op jit(solution)/shard_map/owner/pallas_call | solution.py:1037
